TPU v7x, 256 devices: a whole 4x4x8 slice. The times are simulated.
256 devices in a mesh: zg: 8 (over z), zl: 32 (over x, y, core).
Axes of the slice: x: 4, y: 4, z: 8, core: 2. Of those that a mesh axis runs over, the one named last changes fastest.
Arguments:
- brick_data: float32 [16384, 16, 256], P(('zg', 'zl')), may hold values from -6 to 6
- brick_xy: int32 [2, 16384], P(None, ('zg', 'zl')), may hold values from 0 to 31, as said below
- brick_live: int32 [4, 256], P(None, ('zg', 'zl')), may hold values from 1 to 16, as said below
Outputs:
- pressure_real: float32 [512, 257, 512], P(('zg', 'zl'))
- pressure_imag: float32 [512, 257, 512], P(('zg', 'zl'))
Inputs may be any that keep to these rules, and one draw needn't show every extreme that they name: brick_live[q, d] counts the live slots of owner d in layer q; the live ones are the first; in every layer some owner has all 16 slots live. `brick_xy`: all slots of one brick layer of one z group (live or not) sit at distinct brick positions.
All inputs are finite; a program needn't handle non-finite values.
Results may differ from a plain program's by a relative error of at most 0.00011.
Values sent between devices are 32-bit elements; how exact they have to be, the bound alone decides.
No kernel may reach another device: no remote copies, remote signals or barrier semaphores. Data moves between devices by JAX's collectives and lax.ppermute only.
A program may use at most 64 MiB of HBM per device.

v0:
```python
import math

import jax
import jax.numpy as jnp
from jax import lax
from jax.sharding import PartitionSpec as P

PLANE = 512
ZLOC = 2


SCREEN = 0.25
HIGHEST = lax.Precision.HIGHEST


def swapped(array, axis, distance):
    return lax.ppermute(array, axis, [(i, i ^ 1 << distance) for i in range(lax.axis_size(axis))])


def bit_count(number):
    return number.bit_length() - 1


def reverse_bits(values, digits):
    result = jnp.zeros_like(values)
    for digit in range(digits):
        result = result | (values >> digit & 1) << digits - 1 - digit
    return result


def dft_tables(length, freq_count):
    points = jnp.arange(length, dtype=jnp.int32)[:, None]
    freqs = jnp.arange(freq_count, dtype=jnp.int32)[None, :]
    angles = 2.0 * jnp.pi / length * (points * freqs % length).astype(jnp.float32)
    return (jnp.cos(angles), jnp.sin(angles))


def rotate(values, angles):
    cosine = jnp.cos(angles)
    sine = jnp.sin(angles)
    return (values[0] * cosine + values[1] * sine, values[1] * cosine - values[0] * sine)


def section_angles(z_rows, half, total):
    exponent = z_rows % half * (total // (2 * half))
    return (2.0 * jnp.pi / total * exponent.astype(jnp.float32))[:, None, None]


def combine_pair(mine, theirs, upper, angles):
    summed = (mine[0] + theirs[0], mine[1] + theirs[1])
    turned = rotate((theirs[0] - mine[0], theirs[1] - mine[1]), angles)
    return (jnp.where(upper, turned[0], summed[0]), jnp.where(upper, turned[1], summed[1]))


def local_sections(values, total):
    count = values[0].shape[0]
    shape = values[0].shape
    half = count // 2
    while half >= 1:
        split_real = values[0].reshape((count // (2 * half), 2, half) + shape[1:])
        split_imag = values[1].reshape((count // (2 * half), 2, half) + shape[1:])
        offsets = jnp.arange(half, dtype=jnp.int32) * (total // (2 * half))
        angles = (2.0 * jnp.pi / total * offsets.astype(jnp.float32))[None, :, None, None]
        summed_real = split_real[:, 0] + split_real[:, 1]
        summed_imag = split_imag[:, 0] + split_imag[:, 1]
        turned = rotate(
            (split_real[:, 0] - split_real[:, 1], split_imag[:, 0] - split_imag[:, 1]), angles
        )
        values = (
            jnp.stack([summed_real, turned[0]], axis=1).reshape(shape),
            jnp.stack([summed_imag, turned[1]], axis=1).reshape(shape),
        )
        half = half // 2
    return values


def on_device(brick_data, brick_xy, brick_live):
    layers = brick_live.shape[0]
    capacity = brick_data.shape[0] // layers
    brick = brick_data.shape[1]
    area = brick_data.shape[2]
    zlocal = ZLOC
    per_layer = brick // zlocal
    ngroup = lax.axis_size("zg")
    nplane = lax.axis_size("zl")
    total = zlocal * ngroup * nplane
    width = PLANE
    blocks = width // brick
    kx_count = width // 2 + 1
    group_idx = lax.axis_index("zg")
    plane_idx = lax.axis_index("zl")
    live = (jnp.arange(capacity, dtype=jnp.int32)[None, :] < brick_live).astype(jnp.float32)
    masked = (
        brick_data.reshape(layers, capacity, per_layer, zlocal, area) * live[:, :, None, None, None]
    )
    outgoing = jnp.transpose(masked, (0, 2, 1, 3, 4)).reshape(
        layers * per_layer, capacity, zlocal, area
    )
    block_ids = (
        (brick_xy[1] * blocks + brick_xy[0]).astype(jnp.float32).reshape(layers, 1, capacity)
    )
    block_out = jnp.broadcast_to(block_ids, (layers, per_layer, capacity)).reshape(
        layers * per_layer, capacity
    )
    pieces, places = (
        lax.all_to_all(outgoing, "zl", split_axis=0, concat_axis=0, tiled=True),
        lax.all_to_all(block_out, "zl", split_axis=0, concat_axis=0, tiled=True),
    )
    slot_ids = places.astype(jnp.int32).reshape(-1)
    incoming = jnp.transpose(pieces, (2, 0, 1, 3)).reshape(zlocal, -1, area)
    blockgrid = (
        jnp.zeros((zlocal, blocks * blocks, area), jnp.float32).at[:, slot_ids, :].add(incoming)
    )
    blockgrid = blockgrid.reshape(zlocal, blocks, blocks, brick, brick)
    cos_x, sin_x = dft_tables(width, kx_count)
    cos_x = cos_x.reshape(blocks, brick, kx_count)
    sin_x = sin_x.reshape(blocks, brick, kx_count)
    first_real = jnp.einsum("zabuv,bvk->zkau", blockgrid, cos_x, precision=HIGHEST).reshape(
        zlocal * kx_count, width
    )
    first_imag = -jnp.einsum("zabuv,bvk->zkau", blockgrid, sin_x, precision=HIGHEST).reshape(
        zlocal * kx_count, width
    )
    cos_y, sin_y = dft_tables(width, width)
    second_real = jnp.dot(first_real, cos_y, precision=HIGHEST) + jnp.dot(
        first_imag, sin_y, precision=HIGHEST
    )
    second_imag = jnp.dot(first_imag, cos_y, precision=HIGHEST) - jnp.dot(
        first_real, sin_y, precision=HIGHEST
    )
    values = (
        second_real.reshape(zlocal, kx_count, width),
        second_imag.reshape(zlocal, kx_count, width),
    )
    device = group_idx * nplane + plane_idx
    z_rows = device * zlocal + jnp.arange(zlocal, dtype=jnp.int32)
    gbits = bit_count(ngroup)
    pbits = bit_count(nplane)
    for level in reversed(range(gbits)):
        half = zlocal * nplane * (1 << level)
        theirs = swapped((values[0], values[1]), "zg", level)
        upper = group_idx >> level & 1 == 1
        values = combine_pair(values, theirs, upper, section_angles(z_rows, half, total))
    plane_values = values
    for level in reversed(range(pbits)):
        half = zlocal * (1 << level)
        theirs = swapped((plane_values[0], plane_values[1]), "zl", level)
        upper = plane_idx >> level & 1 == 1
        plane_values = combine_pair(
            plane_values, theirs, upper, section_angles(z_rows, half, total)
        )
    plane_values = local_sections(plane_values, total)
    values = plane_values
    kz_rows = reverse_bits(z_rows, bit_count(total))
    along_z = 4.0 * jnp.sin(jnp.pi * kz_rows.astype(jnp.float32) / total) ** 2
    along_x = 4.0 * jnp.sin(jnp.pi * jnp.arange(kx_count, dtype=jnp.float32) / width) ** 2
    along_y = 4.0 * jnp.sin(jnp.pi * jnp.arange(width, dtype=jnp.float32) / width) ** 2
    denom = along_z[:, None, None] + along_x[None, :, None] + along_y[None, None, :] + SCREEN
    factor = -(1.0 / math.sqrt(width * width * total)) / denom
    return (values[0] * factor, values[1] * factor)


def solution(mesh):
    in_specs = (P(("zg", "zl"), None, None), P(None, ("zg", "zl")), P(None, ("zg", "zl")))
    out_specs = (P(("zg", "zl"), None, None), P(("zg", "zl"), None, None))
    return jax.shard_map(
        on_device, mesh=mesh, in_specs=in_specs, out_specs=out_specs, check_vma=False
    )
```

profile of v0, /device:TPU:1, one launch (start us, length us, event | category | flops | bytes accessed | tf_op | source)
XLA Modules:
  0.0 616.9 jit_solution(15497865746832231019)
XLA Ops:
  2.1 8.6 %all-to-all-start = ((f32[32,1,16]{2,1,0:T(1,128)}), f32[32,1,16]{2,1,0:T(1,128)S(1)}, u32[]{:S(2)}, u32[]{:S(2)}) async-start(f32[32,1,16]{2,1,0:T(1,128)} %bitcast.3), calls=%async_computation | async-start | bytes 32768 | tf_op jit(solution)/shard_map/all_to_all | solution.py:107
  22.1 16.8 %all-to-all-done.1 = f32[32,16,2,256]{3,1,2,0:T(8,128)S(1)} async-done(((f32[32,16,2,256]{3,1,2,0:T(8,128)}), f32[32,16,2,256]{3,1,2,0:T(8,128)S(1)}, u32[]{:S(2)}, u32[]{:S(2)}) %all-to-all-start.1) | async-done | bytes 1048608 | tf_op jit(solution)/shard_map/all_to_all | solution.py:106
  40.3 17.8 %scatter_fusion = f32[2,1024,256]{2,0,1:T(2,128)S(1)} fusion(f32[2,1024,256]{2,0,1:T(2,128)S(1)} %broadcast_in_dim.4, s32[512]{0:T(512)S(1)} %bitcast.64, f32[512,2,256]{2,1,0:T(2,128)S(1)} %copy.30), kind=kCustom, calls=%fused_computation | custom fusion | flops 262144 | bytes 3147776 | tf_op jit(solution)/shard_map/scatter-add | solution.py:112
  67.5 18.7 %fusion = f32[2,257,32,16]{1,2,3,0:T(8,128)S(1)} fusion(f32[2,32,32,16,16]{2,1,4,3,0:T(8,128)} %reshape.487, s32[32,16]{0,1:T(8,128)S(1)} %multiply_add_fusion.1), kind=kOutput, calls=%fused_computation.2 | convolution fusion | flops 1619009536 | bytes 3151872 | tf_op jit(solution)/shard_map/zabuv,bvk->zkau/dot_general | solution.py:121
  86.2 13.1 %convolution_bitcast_fusion = f32[2,257,32,16]{1,2,3,0:T(8,128)S(1)} fusion(f32[2,32,32,16,16]{2,1,4,3,0:T(8,128)S(1)} %copy-done.5, s32[32,16]{0,1:T(8,128)S(1)} %multiply_add_fusion.1), kind=kOutput, calls=%fused_computation.6 | convolution fusion | flops 1618746368 | bytes 3151872 | tf_op jit(solution)/shard_map/zabuv,bvk->zkau/dot_general | solution.py:118
  105.2 8.1 %fusion.21 = f32[514,512]{1,0:T(8,128)S(1)} fusion(f32[514,512]{0,1:T(8,128)S(1)} %neg.11), kind=kOutput, calls=%fused_computation.70 | convolution fusion | flops 1620574208 | bytes 2105344 | tf_op jit(solution)/shard_map/dot_general | solution.py:128
  113.3 8.5 %fusion.23 = f32[514,512]{1,0:T(8,128)S(1)} fusion(f32[514,512]{0,1:T(8,128)S(1)} %copy-done.6), kind=kOutput, calls=%fused_computation.71 | convolution fusion | flops 1620574208 | bytes 2105344 | tf_op jit(solution)/shard_map/dot_general | solution.py:125
  121.9 8.8 %convolution_subtract_fusion = f32[514,512]{1,0:T(8,128)} fusion(f32[514,512]{1,0:T(8,128)S(1)} %fusion.21, f32[514,512]{0,1:T(8,128)S(1)} %copy-done.6), kind=kOutput, calls=%fused_computation.7 | convolution fusion | flops 1620837376 | bytes 3158016 | tf_op jit(solution)/shard_map/dot_general | solution.py:128
  130.7 8.9 %convolution_add_fusion = f32[514,512]{1,0:T(8,128)} fusion(f32[514,512]{1,0:T(8,128)S(1)} %fusion.23, f32[514,512]{0,1:T(8,128)S(1)} %neg.11), kind=kOutput, calls=%fused_computation.8 | convolution fusion | flops 1620837376 | bytes 3158016 | tf_op jit(solution)/shard_map/dot_general | solution.py:125
  151.8 29.6 %collective-permute-done = f32[2,257,512]{2,0,1:T(2,128)S(1)} collective-permute-done((f32[2,257,512]{2,0,1:T(2,128)}, f32[2,257,512]{2,0,1:T(2,128)S(1)}, u32[]{:S(2)}, u32[]{:S(2)}) %collective-permute-start) | collective-permute-done | bytes 1052704 | tf_op jit(solution)/shard_map/ppermute | solution.py:17
  181.3 32.8 %collective-permute-done.1 = f32[2,257,512]{2,0,1:T(2,128)} collective-permute-done((f32[2,257,512]{2,0,1:T(2,128)}, f32[2,257,512]{2,0,1:T(2,128)}, u32[]{:S(2)}, u32[]{:S(2)}) %collective-permute-start.1) | collective-permute-done | bytes 1052704 | tf_op jit(solution)/shard_map/ppermute | solution.py:17
  219.9 30.2 %collective-permute-start.2 = (f32[2,257,512]{2,0,1:T(2,128)}, f32[2,257,512]{2,0,1:T(2,128)S(1)}, u32[]{:S(2)}, u32[]{:S(2)}) collective-permute-start(f32[2,257,512]{2,0,1:T(2,128)} %copy.39), channel_id=1, source_target_pairs={{0,64},{32,96},{64,0},{96,32},{128,192},{160,224},{192,128},{224,1... | collective-permute-start | bytes 3158024 | tf_op jit(solution)/shard_map/ppermute | solution.py:17
  250.2 67.6 %collective-permute-done.2 = f32[2,257,512]{2,0,1:T(2,128)S(1)} collective-permute-done((f32[2,257,512]{2,0,1:T(2,128)}, f32[2,257,512]{2,0,1:T(2,128)S(1)}, u32[]{:S(2)}, u32[]{:S(2)}) %collective-permute-start.2) | collective-permute-done | bytes 1052704 | tf_op jit(solution)/shard_map/ppermute | solution.py:17
  317.9 22.6 %collective-permute-done.3 = f32[2,257,512]{2,0,1:T(2,128)S(1)} collective-permute-done((f32[2,257,512]{2,0,1:T(2,128)}, f32[2,257,512]{2,0,1:T(2,128)S(1)}, u32[]{:S(2)}, u32[]{:S(2)}) %collective-permute-start.3) | collective-permute-done | bytes 1052704 | tf_op jit(solution)/shard_map/ppermute | solution.py:17
  349.1 21.4 %collective-permute-done.4 = f32[2,257,512]{2,0,1:T(2,128)S(1)} collective-permute-done((f32[2,257,512]{2,0,1:T(2,128)}, f32[2,257,512]{2,0,1:T(2,128)S(1)}, u32[]{:S(2)}, u32[]{:S(2)}) %collective-permute-start.4) | collective-permute-done | bytes 1052704 | tf_op jit(solution)/shard_map/ppermute | solution.py:17
  370.6 22.7 %collective-permute-done.5 = f32[2,257,512]{2,0,1:T(2,128)} collective-permute-done((f32[2,257,512]{2,0,1:T(2,128)}, f32[2,257,512]{2,0,1:T(2,128)}, u32[]{:S(2)}, u32[]{:S(2)}) %collective-permute-start.5) | collective-permute-done | bytes 1052704 | tf_op jit(solution)/shard_map/ppermute | solution.py:17
  402.0 20.7 %collective-permute-done.6 = f32[2,257,512]{2,0,1:T(2,128)S(1)} collective-permute-done((f32[2,257,512]{2,0,1:T(2,128)}, f32[2,257,512]{2,0,1:T(2,128)S(1)}, u32[]{:S(2)}, u32[]{:S(2)}) %collective-permute-start.6) | collective-permute-done | bytes 1052704 | tf_op jit(solution)/shard_map/ppermute | solution.py:17
  422.7 22.6 %collective-permute-done.7 = f32[2,257,512]{2,0,1:T(2,128)S(1)} collective-permute-done((f32[2,257,512]{2,0,1:T(2,128)}, f32[2,257,512]{2,0,1:T(2,128)S(1)}, u32[]{:S(2)}, u32[]{:S(2)}) %collective-permute-start.7) | collective-permute-done | bytes 1052704 | tf_op jit(solution)/shard_map/ppermute | solution.py:17
  453.8 19.8 %collective-permute-done.8 = f32[2,257,512]{2,0,1:T(2,128)S(1)} collective-permute-done((f32[2,257,512]{2,0,1:T(2,128)}, f32[2,257,512]{2,0,1:T(2,128)S(1)}, u32[]{:S(2)}, u32[]{:S(2)}) %collective-permute-start.8) | collective-permute-done | bytes 1052704 | tf_op jit(solution)/shard_map/ppermute | solution.py:17
  473.6 22.7 %collective-permute-done.9 = f32[2,257,512]{2,0,1:T(2,128)} collective-permute-done((f32[2,257,512]{2,0,1:T(2,128)}, f32[2,257,512]{2,0,1:T(2,128)}, u32[]{:S(2)}, u32[]{:S(2)}) %collective-permute-start.9) | collective-permute-done | bytes 1052704 | tf_op jit(solution)/shard_map/ppermute | solution.py:17
  505.2 18.6 %collective-permute-done.10 = f32[2,257,512]{2,0,1:T(2,128)S(1)} collective-permute-done((f32[2,257,512]{2,0,1:T(2,128)}, f32[2,257,512]{2,0,1:T(2,128)S(1)}, u32[]{:S(2)}, u32[]{:S(2)}) %collective-permute-start.10) | collective-permute-done | bytes 1052704 | tf_op jit(solution)/shard_map/ppermute | solution.py:17
  523.9 22.6 %collective-permute-done.11 = f32[2,257,512]{2,0,1:T(2,128)S(1)} collective-permute-done((f32[2,257,512]{2,0,1:T(2,128)}, f32[2,257,512]{2,0,1:T(2,128)S(1)}, u32[]{:S(2)}, u32[]{:S(2)}) %collective-permute-start.11) | collective-permute-done | bytes 1052704 | tf_op jit(solution)/shard_map/ppermute | solution.py:17
  552.5 17.9 %collective-permute-done.12 = f32[2,257,512]{2,0,1:T(2,128)S(1)} collective-permute-done((f32[2,257,512]{2,0,1:T(2,128)}, f32[2,257,512]{2,0,1:T(2,128)S(1)}, u32[]{:S(2)}, u32[]{:S(2)}) %collective-permute-start.12) | collective-permute-done | bytes 1052704 | tf_op jit(solution)/shard_map/ppermute | solution.py:17
  570.4 22.6 %collective-permute-done.13 = f32[2,257,512]{2,0,1:T(2,128)S(1)} collective-permute-done((f32[2,257,512]{2,0,1:T(2,128)S(1)}, f32[2,257,512]{2,0,1:T(2,128)S(1)}, u32[]{:S(2)}, u32[]{:S(2)}) %collective-permute-start.13) | collective-permute-done | bytes 1052704 | tf_op jit(solution)/shard_map/ppermute | solution.py:17
  (113 shorter events, 112.0 us)
Async XLA Ops:
  2.1 15.5 %all-to-all-start = ((f32[32,1,16]{2,1,0:T(1,128)}), f32[32,1,16]{2,1,0:T(1,128)S(1)}, u32[]{:S(2)}, u32[]{:S(2)}) async-start(f32[32,1,16]{2,1,0:T(1,128)} %bitcast.3), calls=%async_computation | async-start | bytes 32768 | tf_op jit(solution)/shard_map/all_to_all | solution.py:107
  17.6 21.3 %all-to-all-start.1 = ((f32[32,16,2,256]{3,1,2,0:T(8,128)}), f32[32,16,2,256]{3,1,2,0:T(8,128)S(1)}, u32[]{:S(2)}, u32[]{:S(2)}) async-start(f32[32,16,2,256]{3,1,2,0:T(8,128)} %bitcast.8), calls=%async_computation.1 | async-start | bytes 2097152 | tf_op jit(solution)/shard_map/all_to_all | solution.py:106
  67.5 18.7 %copy-start.5 = (f32[2,32,32,16,16]{2,1,4,3,0:T(8,128)S(1)}, f32[2,32,32,16,16]{2,1,4,3,0:T(8,128)}, u32[]{:S(2)}) copy-start(f32[2,32,32,16,16]{2,1,4,3,0:T(8,128)} %reshape.487) | copy-start | bytes 6291460
  144.8 36.5 %collective-permute-start = (f32[2,257,512]{2,0,1:T(2,128)}, f32[2,257,512]{2,0,1:T(2,128)S(1)}, u32[]{:S(2)}, u32[]{:S(2)}) collective-permute-start(f32[2,257,512]{2,0,1:T(2,128)} %copy.34), channel_id=1, source_target_pairs={{0,128},{32,160},{64,192},{96,224},{128,0},{160,32},{192,64},{224,... | collective-permute-start | bytes 3158024 | tf_op jit(solution)/shard_map/ppermute | solution.py:17
  151.7 62.5 %collective-permute-start.1 = (f32[2,257,512]{2,0,1:T(2,128)}, f32[2,257,512]{2,0,1:T(2,128)}, u32[]{:S(2)}, u32[]{:S(2)}) collective-permute-start(f32[2,257,512]{2,0,1:T(2,128)} %copy.36), channel_id=1, source_target_pairs={{0,128},{32,160},{64,192},{96,224},{128,0},{160,32},{192,64},{224,... | collective-permute-start | bytes 3158024 | tf_op jit(solution)/shard_map/ppermute | solution.py:17
  181.3 32.8 %copy-start.8 = (f32[2,257,512]{2,0,1:T(2,128)}, f32[2,257,512]{2,0,1:T(2,128)S(1)}, u32[]{:S(2)}) copy-start(f32[2,257,512]{2,0,1:T(2,128)S(1)} %collective-permute-done) | copy-start | bytes 3158020
  219.9 98.0 %collective-permute-start.2 = (f32[2,257,512]{2,0,1:T(2,128)}, f32[2,257,512]{2,0,1:T(2,128)S(1)}, u32[]{:S(2)}, u32[]{:S(2)}) collective-permute-start(f32[2,257,512]{2,0,1:T(2,128)} %copy.39), channel_id=1, source_target_pairs={{0,64},{32,96},{64,0},{96,32},{128,192},{160,224},{192,128},{224,1... | collective-permute-start | bytes 3158024 | tf_op jit(solution)/shard_map/ppermute | solution.py:17
  250.1 90.3 %collective-permute-start.3 = (f32[2,257,512]{2,0,1:T(2,128)}, f32[2,257,512]{2,0,1:T(2,128)S(1)}, u32[]{:S(2)}, u32[]{:S(2)}) collective-permute-start(f32[2,257,512]{2,0,1:T(2,128)} %copy.42), channel_id=1, source_target_pairs={{0,64},{32,96},{64,0},{96,32},{128,192},{160,224},{192,128},{224,1... | collective-permute-start | bytes 3158024 | tf_op jit(solution)/shard_map/ppermute | solution.py:17
  317.9 22.6 %copy-start.12 = (f32[2,257,512]{2,0,1:T(2,128)}, f32[2,257,512]{2,0,1:T(2,128)S(1)}, u32[]{:S(2)}) copy-start(f32[2,257,512]{2,0,1:T(2,128)S(1)} %collective-permute-done.2) | copy-start | bytes 3158020
  347.4 23.2 %collective-permute-start.4 = (f32[2,257,512]{2,0,1:T(2,128)}, f32[2,257,512]{2,0,1:T(2,128)S(1)}, u32[]{:S(2)}, u32[]{:S(2)}) collective-permute-start(f32[2,257,512]{2,0,1:T(2,128)} %copy.45), channel_id=1, source_target_pairs={{0,32},{32,0},{64,96},{96,64},{128,160},{160,128},{192,224},{224,1... | collective-permute-start | bytes 3158024 | tf_op jit(solution)/shard_map/ppermute | solution.py:17
  347.4 45.8 %collective-permute-start.5 = (f32[2,257,512]{2,0,1:T(2,128)}, f32[2,257,512]{2,0,1:T(2,128)}, u32[]{:S(2)}, u32[]{:S(2)}) collective-permute-start(f32[2,257,512]{2,0,1:T(2,128)} %copy.48), channel_id=1, source_target_pairs={{0,32},{32,0},{64,96},{96,64},{128,160},{160,128},{192,224},{224,1... | collective-permute-start | bytes 3158024 | tf_op jit(solution)/shard_map/ppermute | solution.py:17
  370.6 22.7 %copy-start.9 = (f32[2,257,512]{2,0,1:T(2,128)}, f32[2,257,512]{2,0,1:T(2,128)S(1)}, u32[]{:S(2)}) copy-start(f32[2,257,512]{2,0,1:T(2,128)S(1)} %collective-permute-done.4) | copy-start | bytes 3158020
  399.0 23.7 %collective-permute-start.6 = (f32[2,257,512]{2,0,1:T(2,128)}, f32[2,257,512]{2,0,1:T(2,128)S(1)}, u32[]{:S(2)}, u32[]{:S(2)}) collective-permute-start(f32[2,257,512]{2,0,1:T(2,128)} %copy.51), channel_id=1, source_target_pairs={{0,16},{1,17},{2,18},{3,19},{4,20},{5,21},{6,22},{7,23},{8,24},{9,... | collective-permute-start | bytes 3158024 | tf_op jit(solution)/shard_map/ppermute | solution.py:17
  401.1 44.2 %collective-permute-start.7 = (f32[2,257,512]{2,0,1:T(2,128)}, f32[2,257,512]{2,0,1:T(2,128)S(1)}, u32[]{:S(2)}, u32[]{:S(2)}) collective-permute-start(f32[2,257,512]{2,0,1:T(2,128)} %copy.54), channel_id=1, source_target_pairs={{0,16},{1,17},{2,18},{3,19},{4,20},{5,21},{6,22},{7,23},{8,24},{9,... | collective-permute-start | bytes 3158024 | tf_op jit(solution)/shard_map/ppermute | solution.py:17
  422.7 22.6 %copy-start.10 = (f32[2,257,512]{2,0,1:T(2,128)}, f32[2,257,512]{2,0,1:T(2,128)S(1)}, u32[]{:S(2)}) copy-start(f32[2,257,512]{2,0,1:T(2,128)S(1)} %collective-permute-done.6) | copy-start | bytes 3158020
  452.3 21.3 %collective-permute-start.8 = (f32[2,257,512]{2,0,1:T(2,128)}, f32[2,257,512]{2,0,1:T(2,128)S(1)}, u32[]{:S(2)}, u32[]{:S(2)}) collective-permute-start(f32[2,257,512]{2,0,1:T(2,128)} %copy.57), channel_id=1, source_target_pairs={{0,8},{1,9},{2,10},{3,11},{4,12},{5,13},{6,14},{7,15},{8,0},{9,1},... | collective-permute-start | bytes 3158024 | tf_op jit(solution)/shard_map/ppermute | solution.py:17
  453.4 42.8 %collective-permute-start.9 = (f32[2,257,512]{2,0,1:T(2,128)}, f32[2,257,512]{2,0,1:T(2,128)}, u32[]{:S(2)}, u32[]{:S(2)}) collective-permute-start(f32[2,257,512]{2,0,1:T(2,128)} %copy.60), channel_id=1, source_target_pairs={{0,8},{1,9},{2,10},{3,11},{4,12},{5,13},{6,14},{7,15},{8,0},{9,1},... | collective-permute-start | bytes 3158024 | tf_op jit(solution)/shard_map/ppermute | solution.py:17
  473.6 22.7 %copy-start.11 = (f32[2,257,512]{2,0,1:T(2,128)}, f32[2,257,512]{2,0,1:T(2,128)S(1)}, u32[]{:S(2)}) copy-start(f32[2,257,512]{2,0,1:T(2,128)S(1)} %collective-permute-done.8) | copy-start | bytes 3158020
  502.0 21.9 %collective-permute-start.10 = (f32[2,257,512]{2,0,1:T(2,128)}, f32[2,257,512]{2,0,1:T(2,128)S(1)}, u32[]{:S(2)}, u32[]{:S(2)}) collective-permute-start(f32[2,257,512]{2,0,1:T(2,128)} %copy.63), channel_id=1, source_target_pairs={{0,4},{1,5},{2,6},{3,7},{4,0},{5,1},{6,2},{7,3},{8,12},{9,13},{10,... | collective-permute-start | bytes 3158024 | tf_op jit(solution)/shard_map/ppermute | solution.py:17
  502.2 44.2 %collective-permute-start.11 = (f32[2,257,512]{2,0,1:T(2,128)}, f32[2,257,512]{2,0,1:T(2,128)S(1)}, u32[]{:S(2)}, u32[]{:S(2)}) collective-permute-start(f32[2,257,512]{2,0,1:T(2,128)} %copy.66), channel_id=1, source_target_pairs={{0,4},{1,5},{2,6},{3,7},{4,0},{5,1},{6,2},{7,3},{8,12},{9,13},{10,... | collective-permute-start | bytes 3158024 | tf_op jit(solution)/shard_map/ppermute | solution.py:17
  550.9 19.5 %collective-permute-start.12 = (f32[2,257,512]{2,0,1:T(2,128)}, f32[2,257,512]{2,0,1:T(2,128)S(1)}, u32[]{:S(2)}, u32[]{:S(2)}) collective-permute-start(f32[2,257,512]{2,0,1:T(2,128)} %copy.69), channel_id=1, source_target_pairs={{0,2},{1,3},{2,0},{3,1},{4,6},{5,7},{6,4},{7,5},{8,10},{9,11},{10,... | collective-permute-start | bytes 3158024 | tf_op jit(solution)/shard_map/ppermute | solution.py:17
  552.3 40.6 %collective-permute-start.13 = (f32[2,257,512]{2,0,1:T(2,128)S(1)}, f32[2,257,512]{2,0,1:T(2,128)S(1)}, u32[]{:S(2)}, u32[]{:S(2)}) collective-permute-start(f32[2,257,512]{2,0,1:T(2,128)S(1)} %copy.72), channel_id=1, source_target_pairs={{0,2},{1,3},{2,0},{3,1},{4,6},{5,7},{6,4},{7,5},{8,10},{9,11},{10,... | collective-permute-start | bytes 3158024 | tf_op jit(solution)/shard_map/ppermute | solution.py:17
  599.9 10.0 %collective-permute-start.14 = (f32[2,257,512]{2,0,1:T(2,128)}, f32[2,257,512]{2,0,1:T(2,128)S(1)}, u32[]{:S(2)}, u32[]{:S(2)}) collective-permute-start(f32[2,257,512]{2,0,1:T(2,128)} %copy.75), channel_id=1, source_target_pairs={{0,1},{1,0},{2,3},{3,2},{4,5},{5,4},{6,7},{7,6},{8,9},{9,8},{10,11... | collective-permute-start | bytes 3158024 | tf_op jit(solution)/shard_map/ppermute | solution.py:17
  606.3 4.1 collective-permute-start.15
  (10 other events, 28.6 us)
where the time goes:
time: 628 us; the launch traced here: 617 us
  waiting for transfers between devices  388 us (62%)
  starting transfers between devices  67.4 us (11%)
  matrix products  66.1 us (11%)
  local copies, waits for them, and re-layouts  56.2 us (9%)
  other arithmetic  38.2 us (6%)
    ppermute x16, waiting for transfers between devices, swapped(): lax.ppermute(array, axis, [(i, i ^ 1 << distance) for i in range(lax.axis...  368 us
    ppermute x16, starting transfers between devices, swapped(): lax.ppermute(array, axis, [(i, i ^ 1 << distance) for i in range(lax.axis...  54.4 us
    dot_general x1, matrix products, on_device(): jnp.einsum('zabuv,bvk->zkau', blockgrid, sin_x, precision=HIGHEST)  18.7 us
    scatter-add x1, other arithmetic, on_device(): jnp.zeros((zlocal, blocks * blocks, area), jnp.float32).at[:, slot_ids, :]  17.8 us
    all_to_all x1, waiting for transfers between devices, on_device(): lax.all_to_all(outgoing, 'zl', split_axis=0, concat_axis=0, tiled=True)  16.8 us
    select_n x7, other arithmetic, combine_pair(): jnp.where(upper, turned[1], summed[1])  15.6 us
    dot_general x1, matrix products, on_device(): jnp.einsum('zabuv,bvk->zkau', blockgrid, cos_x, precision=HIGHEST)  13.1 us
  transfers between devices with their start and end apart: 18, of which 18 were waited for; matrix products, arithmetic and copies ran while one was open for 1% of the time, Pallas kernels for 0%

commit v1 on v0

v1 whole, which is shorter than its diff:
```python
import math

import jax
import jax.numpy as jnp
import numpy as np
from jax import lax
from jax.experimental import pallas as pl
from jax.experimental.pallas import tpu as pltpu
from jax.sharding import PartitionSpec as P

AXES = ("zg", "zl")
NZ = 512
PLANE = 512
BRICK = 16
BLOCKS = 32
LAYERS = 4
CAP = 16
GROUPS = 8
DEVICES = 256
KX = 257
SLOTS = LAYERS * CAP
SITES = BLOCKS * BLOCKS
SCREEN = 0.25
BF16 = jnp.bfloat16
F32 = jnp.float32


def reverse_bits(values, digits):
    result = values * 0
    for digit in range(digits):
        result = result | ((values >> digit) & 1) << (digits - 1 - digit)
    return result


def halves_np(table):
    high = table.astype(np.float32).astype(jnp.bfloat16)
    low = (table - high.astype(np.float64)).astype(np.float32).astype(jnp.bfloat16)
    return high, low


def lattice_tables():
    bx, by = np.divmod(np.arange(SITES), BLOCKS)
    kx, ky = np.divmod(np.arange(SITES), BLOCKS)
    turn = (bx[:, None] * kx[None, :] + by[:, None] * ky[None, :]) % BLOCKS
    angle = 2.0 * np.pi * turn / BLOCKS
    return halves_np(np.concatenate([np.cos(angle), -np.sin(angle)], axis=1))


def depth_tables():
    device = np.arange(DEVICES)
    kz = reverse_bits(2 * device, 9)
    q, g, zh = np.meshgrid(np.arange(LAYERS), np.arange(GROUPS), np.arange(8), indexing="ij")
    tables = []
    for parity in range(2):
        z = (g * 64 + q * 16 + 2 * zh + parity).reshape(-1)
        angle = 2.0 * np.pi * (kz[:, None] * z[None, :] % NZ) / NZ
        cos, sin = np.cos(angle), np.sin(angle)
        tables.append(np.block([[cos, sin], [-sin, cos]]))
    return halves_np(np.stack(tables))


def cell_tables():
    yy, xx = np.divmod(np.arange(DEVICES), BRICK)

    def block(k1y, k1x):
        angle = 2.0 * np.pi * ((k1y[:, None] * yy + k1x[:, None] * xx) % BRICK) / BRICK
        cos, sin = np.cos(angle), np.sin(angle)
        return np.block([[cos, sin], [-sin, cos]])

    t, j, k1x = (a.reshape(-1) for a in np.meshgrid(np.arange(4), np.arange(4), np.arange(8), indexing="ij"))
    main = block(4 * t + j, k1x)
    j, t = (a.reshape(-1) for a in np.meshgrid(np.arange(4), np.arange(8), indexing="ij"))
    last = block(4 * (t % 4) + j, np.full(32, 8))
    return halves_np(np.concatenate([main, last], axis=0))


def lap_tables():
    along_x = 4.0 * np.sin(np.pi * np.arange(288) / PLANE) ** 2
    along_y = 4.0 * np.sin(np.pi * np.arange(PLANE) / PLANE) ** 2
    rows = along_x[:256].reshape(8, 32).T
    lap_x = np.broadcast_to(rows[:, :, None], (32, 8, 128)).astype(np.float32)
    lap_y = np.broadcast_to(along_y.reshape(4, 1, 128), (4, 8, 128)).astype(np.float32)
    return lap_x, lap_y


def split(values):
    high = values.astype(BF16)
    return high, (values - high.astype(F32)).astype(BF16)


def dot(a, b):
    return jnp.dot(a, b, preferred_element_type=F32)


def dot3(a_high, a_low, b_high, b_low):
    return dot(a_high, b_high) + dot(a_high, b_low) + dot(a_low, b_high)


def middle_kernel(
    cells, places, twiddle, lat_high, lat_low, dep_high, dep_low, out, field_high, field_low
):
    lane_group = lax.broadcasted_iota(jnp.int32, (8, DEVICES), 1) // 32
    site = lax.broadcasted_iota(jnp.int32, (DEVICES, SITES), 1).astype(F32)

    def place_layer(q, _):
        where = places[q]
        total = jnp.zeros((256, SITES), F32)
        for c in range(CAP):
            rows = []
            for parity in range(2):
                at = pl.multiple_of(q * 256 + c * 16 + parity * 8, 8)
                rows.append(cells[pl.ds(at, 8), :])
            tops = [r.astype(BF16).astype(F32) for r in rows]
            lows = [r - t for r, t in zip(rows, tops)]
            pieces = [
                jnp.where(lane_group == g, part, 0.0)
                for part in tops + lows
                for g in range(GROUPS)
            ]
            spread = jnp.concatenate(pieces, axis=0).astype(BF16)
            chosen = jnp.where(where[:, c : c + 1] == site, 1.0, 0.0).astype(BF16)
            total = total + dot(spread, chosen)
        layer = total[:128] + total[128:]
        high, low = split(layer)
        for parity in range(2):
            at = pl.multiple_of(parity * 256 + q * 64, 64)
            field_high[pl.ds(at, 64), :] = high[parity * 64 : parity * 64 + 64]
            field_low[pl.ds(at, 64), :] = low[parity * 64 : parity * 64 + 64]
        return 0

    lax.fori_loop(0, LAYERS, place_layer, 0)

    def columns(tile, _):
        at = pl.multiple_of(tile * 256, 256)
        parts = []
        for ri in range(2):
            from_col = pl.ds(pl.multiple_of(ri * SITES + at, 256), 256)
            parts.append(
                dot3(
                    field_high[...], field_low[...], lat_high[:, from_col], lat_low[:, from_col]
                )
            )
        turn_re = twiddle[0:1, pl.ds(at, 256)]
        turn_im = twiddle[1:2, pl.ds(at, 256)]
        real = parts[0] * turn_re - parts[1] * turn_im
        imag = parts[0] * turn_im + parts[1] * turn_re
        sums = []
        for parity in range(2):
            rows = slice(parity * 256, parity * 256 + 256)
            high, low = split(jnp.concatenate([real[rows], imag[rows]], axis=0))
            sums.append(dot3(dep_high[parity], dep_low[parity], high, low))
        for b in range(2):
            both = sums[0] + sums[1] if b == 0 else sums[0] - sums[1]
            for ri in range(2):
                for h in range(2):
                    out[pl.ds((b * 2 + ri) * 8 + tile * 2 + h, DEVICES, stride=32), :] = both[
                        ri * 256 : ri * 256 + 256, h * 128 : h * 128 + 128
                    ]
        return 0

    lax.fori_loop(0, SITES // 256, columns, 0)


def middle(cells, places, twiddle):
    tables = [jnp.asarray(t) for t in (*lattice_tables(), *depth_tables())]
    return pl.pallas_call(
        middle_kernel,
        out_shape=jax.ShapeDtypeStruct((DEVICES * 32, 128), F32),
        in_specs=[pl.BlockSpec(memory_space=pltpu.VMEM)] * 7,
        out_specs=pl.BlockSpec(memory_space=pltpu.VMEM),
        scratch_shapes=[pltpu.VMEM((NZ, SITES), BF16), pltpu.VMEM((NZ, SITES), BF16)],
        compiler_params=pltpu.CompilerParams(vmem_limit_bytes=56 << 20),
        name="middle",
    )(cells, places, twiddle, *tables)


def final_kernel(pieces, lap_z, lap_x, lap_y, cell_high, cell_low, out_re, out_im, rows_ref):
    block = lax.broadcasted_iota(jnp.int32, (8, 128), 1) // 32
    scale = -1.0 / math.sqrt(PLANE * PLANE * NZ)
    outs = (out_re, out_im)

    def group(step, _):
        b = step // 4
        pair = step % 4
        parts = []
        for ri in range(2):
            halves = [
                pieces[pl.ds((b * 2 + ri) * 8 + pair * 2 + h, DEVICES, stride=32), :]
                for h in range(2)
            ]
            parts.append(jnp.concatenate(halves, axis=1))
        high, low = split(jnp.concatenate(parts, axis=0))
        result = dot3(cell_high[0:256, :], cell_low[0:256, :], high, low)
        along_z = lap_z[b]
        for h in range(2):
            for t in range(4):
                tiles = []
                for ri in range(2):
                    at = ri * 128 + t * 32
                    row = [
                        result[at + j * 8 : at + j * 8 + 8, h * 128 : h * 128 + 128]
                        for j in range(4)
                    ]
                    tiles.append(transpose_blocks(row, block))
                for r in range(4):
                    kx = (pair * 2 + h) * 4 + r
                    factor = scale / (along_z + lap_x[kx] + lap_y[t] + SCREEN)
                    for ri in range(2):
                        rows_ref[pl.ds((ri * 4 + t) * 256 + kx, 8, stride=32), :] = (
                            tiles[ri][r] * factor
                        )

        @pl.when(pair == 0)
        def _():
            last = dot3(cell_high[256:320, :], cell_low[256:320, :], high[:, :128], low[:, :128])
            for ri in range(2):
                line = jnp.zeros((8, 128), F32)
                for j in range(4):
                    part = last[ri * 32 + j * 8 : ri * 32 + j * 8 + 8, :]
                    moved = part if j == 0 else pltpu.roll(part, 32 * j, 1)
                    line = jnp.where(block == j, moved, line)
                for t in range(4):
                    factor = scale / (along_z[0:1] + 4.0 + lap_y[t, 0:1] + SCREEN)
                    outs[ri][b, 256:257, t * 128 : t * 128 + 128] = line[t : t + 1] * factor

        @pl.when(pair == 3)
        def _():
            for ri in range(2):
                for t in range(4):
                    at = (ri * 4 + t) * 256
                    outs[ri][b, 0:256, t * 128 : t * 128 + 128] = rows_ref[at : at + 256, :]

        return 0

    lax.fori_loop(0, 8, group, 0)


def transpose_blocks(row, block):
    tiles = []
    for r in range(4):
        tile = row[r]
        for j in range(4):
            if j != r:
                tile = jnp.where(block == j, pltpu.roll(row[j], (32 * (j - r)) % 128, 1), tile)
        tiles.append(tile)
    return tiles


def final(pieces, lap_z):
    lap_x, lap_y = lap_tables()
    tables = [jnp.asarray(t) for t in (lap_x, lap_y, *cell_tables())]
    shape = jax.ShapeDtypeStruct((2, KX, PLANE), F32)
    return pl.pallas_call(
        final_kernel,
        out_shape=(shape, shape),
        in_specs=[pl.BlockSpec(memory_space=pltpu.VMEM)] * 6,
        out_specs=(pl.BlockSpec(memory_space=pltpu.VMEM), pl.BlockSpec(memory_space=pltpu.VMEM)),
        scratch_shapes=[pltpu.VMEM((8 * 256, 128), F32)],
        compiler_params=pltpu.CompilerParams(vmem_limit_bytes=56 << 20),
        name="final",
    )(pieces, lap_z, *tables)


def twiddle_of(device):
    yy = device // BRICK
    xx = device % BRICK
    column = jnp.arange(SITES, dtype=jnp.int32)
    turn = ((column // BLOCKS) * xx + (column % BLOCKS) * yy) % PLANE
    angle = (2.0 * math.pi / PLANE) * turn.astype(F32)
    return jnp.stack([jnp.cos(angle), -jnp.sin(angle)])


def lap_z_of(device):
    kz = reverse_bits(2 * device + jnp.arange(2, dtype=jnp.int32), 9)
    along_z = 4.0 * jnp.sin(math.pi * kz.astype(F32) / NZ) ** 2
    return jnp.broadcast_to(along_z[:, None, None], (2, 8, 128))


def on_device(brick_data, brick_xy, brick_live):
    device = lax.axis_index("zg") * 32 + lax.axis_index("zl")
    live = jnp.arange(CAP, dtype=jnp.int32)[None, :] < brick_live
    place = (brick_xy[0] * BLOCKS + brick_xy[1]).astype(F32).reshape(LAYERS, CAP)
    place = jnp.where(live, place, -1.0).reshape(SLOTS, 1)
    by_parity = jnp.swapaxes(brick_data.reshape(SLOTS, 8, 2, 256), 1, 2)
    outgoing = jnp.concatenate(
        [by_parity.reshape(SLOTS * BRICK, 256), jnp.broadcast_to(place, (SLOTS, 256))], axis=0
    )
    sent = outgoing.T.reshape(DEVICES, 1, SLOTS * (BRICK + 1))
    got = lax.all_to_all(sent, AXES, 0, 0, tiled=True).reshape(DEVICES, SLOTS * (BRICK + 1))
    cells = got[:, : SLOTS * BRICK].T
    places = got[:, SLOTS * BRICK :].reshape(DEVICES, LAYERS, CAP).transpose(1, 0, 2)
    rows = middle(cells, places, twiddle_of(device))
    pieces = lax.all_to_all(rows.reshape(DEVICES, 32, 128), AXES, 0, 0, tiled=True)
    return final(pieces.reshape(DEVICES * 32, 128), lap_z_of(device))


def solution(mesh):
    in_specs = (P(AXES, None, None), P(None, AXES), P(None, AXES))
    out_specs = (P(AXES, None, None), P(AXES, None, None))
    return jax.shard_map(
        on_device, mesh=mesh, in_specs=in_specs, out_specs=out_specs, check_vma=False
    )
```

time: 628 us -> 211 us (0.34); the launches traced: 617 us -> 210 us
  waiting for transfers between devices: 388 us -> 129 us
  matrix products: 66.1 us -> 0 us
  starting transfers between devices: 67.4 us -> 23.7 us
  local copies, waits for them, and re-layouts: 56.2 us -> 14.7 us
  Pallas kernels: 0 us -> 41.1 us
  other arithmetic: 38.2 us -> 1.11 us
    ppermute x16 -> x0, waiting for transfers between devices: 368 us -> none  [swapped(): lax.ppermute(array, axis, [(i, i ^ 1 << distance) for i in range(lax.axis...]
    all_to_all x2, waiting for transfers between devices: 19.8 us -> 129 us  [the longest x1 96.6 us: on_device(): lax.all_to_all(rows.reshape(DEVICES, 32, 128), AXES, 0, 0, tiled=True)]
    dot_general x6 -> x0, matrix products: 66.1 us -> none  [the longest x1 18.7 us: on_device(): jnp.einsum('zabuv,bvk->zkau', blockgrid, sin_x, precision=HIGHEST)]
    ppermute x16 -> x0, starting transfers between devices: 54.4 us -> none  [swapped(): lax.ppermute(array, axis, [(i, i ^ 1 << distance) for i in range(lax.axis...]
    pallas_call x0 -> x2, Pallas kernels: none -> 41.1 us  [the longest x1 29.5 us: middle(): pl.pallas_call(middle_kernel, out_shape=jax.ShapeDtypeStruct((DEVICES * 3...]
    select_n x14 -> x0, local copies, waits for them, and re-layouts: 24 us -> none  [the longest x7 12.5 us: combine_pair(): jnp.where(upper, turned[0], summed[0])]
    scatter-add x1 -> x0, other arithmetic: 17.8 us -> none  [on_device(): jnp.zeros((zlocal, blocks * blocks, area), jnp.float32).at[:, slot_ids, :]]
    select_n x8 -> x1, other arithmetic: 15.7 us -> 0.01 us  [on_device(): place = jnp.where(live, place, -1.0).reshape(SLOTS, 1)]
  transfers between devices with their start and end apart: 18 -> 2, of which waited for: 18 -> 2; matrix products, arithmetic and copies ran while one was open for 1% -> 0% of each run, Pallas kernels for 0% -> 0%
where the time goes in v1:
time: 211 us; the launch traced here: 210 us
  waiting for transfers between devices  129 us (61%)
  Pallas kernels  41.1 us (19%)
  starting transfers between devices  23.7 us (11%)
  local copies, waits for them, and re-layouts  14.7 us (7%)
    all_to_all x1, waiting for transfers between devices, on_device(): lax.all_to_all(rows.reshape(DEVICES, 32, 128), AXES, 0, 0, tiled=True)  96.6 us
    all_to_all x1, waiting for transfers between devices, on_device(): lax.all_to_all(sent, AXES, 0, 0, tiled=True)  32.5 us
    pallas_call x1, Pallas kernels, middle(): pl.pallas_call(middle_kernel, out_shape=jax.ShapeDtypeStruct((DEVICES * 3...  29.5 us
    all_to_all x1, starting transfers between devices, on_device(): lax.all_to_all(sent, AXES, 0, 0, tiled=True)  15.7 us
    pallas_call x1, Pallas kernels, final(): pl.pallas_call(final_kernel, out_shape=(shape, shape), in_specs=[pl.Block...  11.6 us
    all_to_all x1, starting transfers between devices, on_device(): lax.all_to_all(rows.reshape(DEVICES, 32, 128), AXES, 0, 0, tiled=True)  8.08 us
    pallas_call x2, local copies, waits for them, and re-layouts, final(): pl.pallas_call(final_kernel, out_shape=(shape, shape), in_specs=[pl.Block...  4.89 us
  transfers between devices with their start and end apart: 2, of which 2 were waited for; matrix products, arithmetic and copies ran while one was open for 0% of the time, Pallas kernels for 0%

profile of v1, /device:TPU:1, one launch (start us, length us, event | category | flops | bytes accessed | tf_op | source)
XLA Modules:
  0.0 210.5 jit_solution(8770282625773550274)
XLA Ops:
  0.6 1.8 copy.30
  2.5 0.0 copy-start.2
  2.5 0.0 copy-start.1
  2.5 0.6 copy.31
  3.1 0.0 copy-done.2
  3.1 0.1 iota_compare_fusion
  3.2 0.1 lt.42
  3.3 0.2 maximum_bitcast_fusion
  3.5 2.7 %copy.32 = f32[256,1,1088]{2,1,0:T(1,128)} copy(f32[256,1,1088]{0,2,1:T(8,128)S(1)} %maximum_bitcast_fusion) | data formatting | bytes 2228224 | tf_op jit(solution)/shard_map/reshape | solution.py:288
  6.3 15.7 %all-to-all-start = ((f32[256,1,1088]{2,1,0:T(1,128)}), f32[256,1,1088]{2,1,0:T(1,128)S(1)}, u32[]{:S(2)}, u32[]{:S(2)}) async-start(f32[256,1,1088]{2,1,0:T(1,128)} %copy.32), calls=%async_computation | async-start | bytes 2359296 | tf_op jit(solution)/shard_map/all_to_all | solution.py:289
  21.9 0.2 sine_negate_fusion
  22.1 0.6 pad_maximum_fusion.twiddle
  22.7 32.5 %all-to-all-done = f32[256,1,1088]{2,1,0:T(1,128)S(1)} async-done(((f32[256,1,1088]{2,1,0:T(1,128)}), f32[256,1,1088]{2,1,0:T(1,128)S(1)}, u32[]{:S(2)}, u32[]{:S(2)}) %all-to-all-start) | async-done | bytes 1114144 | tf_op jit(solution)/shard_map/all_to_all | solution.py:289
  55.2 1.8 copy.33
  57.0 1.0 slice_bitcast_fusion.cells
  58.1 1.0 copy.34
  59.1 29.5 %middle.1 = f32[8192,128]{1,0:T(8,128)} custom-call(f32[1024,256]{1,0:T(8,128)} %slice_bitcast_fusion.cells, f32[4,256,16]{2,1,0:T(8,128)} %bitcast.23, f32[2,1024]{1,0:T(2,128)} %pad_maximum_fusion.twiddle, bf16[1024,2048]{1,0:T(8,128)(2,1)} %constant.119.clone.lat_high, bf16[1024,2048]{1,0:T(8,128)(2,1)} %constant.120.clone.lat_low, ...), custom_call_target="tpu_custom_call" | custom-call | tf_op jit(solution)/shard_map/middle/pallas_call | solution.py:166
  88.6 8.1 %all-to-all-start.1 = ((f32[256,32,128]{2,1,0:T(8,128)}), f32[256,32,128]{2,1,0:T(8,128)}, u32[]{:S(2)}, u32[]{:S(2)}) async-start(f32[256,32,128]{2,1,0:T(8,128)} %bitcast.18), calls=%async_computation.1 | async-start | bytes 8388608 | tf_op jit(solution)/shard_map/all_to_all | solution.py:293
  96.6 0.1 multiply_multiply_fusion
  96.7 96.6 %all-to-all-done.1 = f32[256,32,128]{2,1,0:T(8,128)} async-done(((f32[256,32,128]{2,1,0:T(8,128)}), f32[256,32,128]{2,1,0:T(8,128)}, u32[]{:S(2)}, u32[]{:S(2)}) %all-to-all-start.1) | async-done | bytes 4194336 | tf_op jit(solution)/shard_map/all_to_all | solution.py:293
  193.3 0.7 broadcast_in_dim.18.lap_z
  193.9 11.6 %final.1 = (f32[2,257,512]{2,1,0:T(8,128)}, f32[2,257,512]{2,1,0:T(8,128)}) custom-call(f32[8192,128]{1,0:T(8,128)} %bitcast.12.pieces, f32[2,8,128]{2,1,0:T(8,128)} %broadcast_in_dim.18.lap_z, f32[32,8,128]{2,1,0:T(8,128)} %constant.123.clone.lap_x, f32[4,8,128]{2,1,0:T(8,128)} %constant.124.clone.lap_y, bf16[320,512]{1,0:T(8,128)(2,1)} %constant.125.clone.cell_high, ...), custom_call_target="tpu_custom_call" | custom-call | tf_op jit(solution)/shard_map/final/pallas_call | solution.py:253
  205.6 3.1 %copy.35 = f32[2,257,512]{2,0,1:T(2,128)} copy(f32[2,257,512]{2,1,0:T(8,128)} %get-tuple-element.10) | data formatting | bytes 2105344 | tf_op jit(solution)/shard_map/final/pallas_call | solution.py:253
  208.7 1.8 copy.36
  (6 shorter events, 0.0 us)
Async XLA Ops:
  2.5 0.7 copy-start.2
  2.5 0.8 copy-start.1
  6.3 48.9 %all-to-all-start = ((f32[256,1,1088]{2,1,0:T(1,128)}), f32[256,1,1088]{2,1,0:T(1,128)S(1)}, u32[]{:S(2)}, u32[]{:S(2)}) async-start(f32[256,1,1088]{2,1,0:T(1,128)} %copy.32), calls=%async_computation | async-start | bytes 2359296 | tf_op jit(solution)/shard_map/all_to_all | solution.py:289
  88.6 104.7 %all-to-all-start.1 = ((f32[256,32,128]{2,1,0:T(8,128)}), f32[256,32,128]{2,1,0:T(8,128)}, u32[]{:S(2)}, u32[]{:S(2)}) async-start(f32[256,32,128]{2,1,0:T(8,128)} %bitcast.18), calls=%async_computation.1 | async-start | bytes 8388608 | tf_op jit(solution)/shard_map/all_to_all | solution.py:293
  205.6 3.1 %copy-start = (f32[2,257,512]{2,1,0:T(8,128)S(1)}, f32[2,257,512]{2,1,0:T(8,128)}, u32[]{:S(2)}) copy-start(f32[2,257,512]{2,1,0:T(8,128)} %get-tuple-element.11) | copy-start | bytes 3158020

commit v2 on v1

--- a/solution.py
+++ b/solution.py
@@ -21,6 +21,7 @@
 SLOTS = LAYERS * CAP
 SITES = BLOCKS * BLOCKS
 SCREEN = 0.25
+CHUNK = 9
 BF16 = jnp.bfloat16
 F32 = jnp.float32
 
@@ -96,28 +97,59 @@
     return dot(a_high, b_high) + dot(a_high, b_low) + dot(a_low, b_high)
 
 
+def send_kernel(bricks, place, out):
+    for h in range(2):
+        for i in range(8):
+            block = bricks[i * 128 : i * 128 + 128, h * 128 : h * 128 + 128]
+            out[pl.ds(h * 128 * CHUNK + i, 128, stride=CHUNK), :] = block.T
+    out[pl.ds(8, DEVICES, stride=CHUNK), :] = jnp.broadcast_to(place[...], (DEVICES, 128))
+
+
+def send(bricks, place):
+    return pl.pallas_call(
+        send_kernel,
+        out_shape=jax.ShapeDtypeStruct((DEVICES * CHUNK, 128), F32),
+        in_specs=[pl.BlockSpec(memory_space=pltpu.VMEM)] * 2,
+        out_specs=pl.BlockSpec(memory_space=pltpu.VMEM),
+        compiler_params=pltpu.CompilerParams(vmem_limit_bytes=56 << 20),
+        name="send",
+    )(bricks, place)
+
+
 def middle_kernel(
-    cells, places, twiddle, lat_high, lat_low, dep_high, dep_low, out, field_high, field_low
+    got, twiddle, lat_high, lat_low, dep_high, dep_low, out, field_high, field_low, cells, places
 ):
-    lane_group = lax.broadcasted_iota(jnp.int32, (8, DEVICES), 1) // 32
+    lane_group = lax.broadcasted_iota(jnp.int32, (8, 128), 1) // 32
+    none = jnp.zeros((8, 128), F32)
+    for i in range(8):
+        block = got[pl.ds(i, DEVICES, stride=CHUNK), :].T
+        for h in range(2):
+            at = h * 1024 + i * 128
+            cells[at : at + 128, :] = block[:, h * 128 : h * 128 + 128]
+    codes = got[pl.ds(8, DEVICES, stride=CHUNK), :]
+    for q in range(LAYERS):
+        places[q] = codes if q == 0 else pltpu.roll(codes, 128 - q * CAP, 1)
     site = lax.broadcasted_iota(jnp.int32, (DEVICES, SITES), 1).astype(F32)
 
     def place_layer(q, _):
         where = places[q]
         total = jnp.zeros((256, SITES), F32)
         for c in range(CAP):
-            rows = []
+            pieces = {}
             for parity in range(2):
-                at = pl.multiple_of(q * 256 + c * 16 + parity * 8, 8)
-                rows.append(cells[pl.ds(at, 8), :])
-            tops = [r.astype(BF16).astype(F32) for r in rows]
-            lows = [r - t for r, t in zip(rows, tops)]
-            pieces = [
-                jnp.where(lane_group == g, part, 0.0)
-                for part in tops + lows
-                for g in range(GROUPS)
-            ]
-            spread = jnp.concatenate(pieces, axis=0).astype(BF16)
+                for h in range(2):
+                    row = cells[pl.ds(h * 1024 + q * 256 + c * 16 + parity, 8, stride=2), :]
+                    top = row.astype(BF16).astype(F32)
+                    pieces[0, parity, h] = top
+                    pieces[1, parity, h] = row - top
+            spread = []
+            for part in range(2):
+                for parity in range(2):
+                    for g in range(GROUPS):
+                        own = jnp.where(lane_group == g % 4, pieces[part, parity, g // 4], 0.0)
+                        pair = [own, none] if g < 4 else [none, own]
+                        spread.append(jnp.concatenate(pair, axis=1))
+            spread = jnp.concatenate(spread, axis=0).astype(BF16)
             chosen = jnp.where(where[:, c : c + 1] == site, 1.0, 0.0).astype(BF16)
             total = total + dot(spread, chosen)
         layer = total[:128] + total[128:]
@@ -161,20 +193,25 @@
     lax.fori_loop(0, SITES // 256, columns, 0)
 
 
-def middle(cells, places, twiddle):
+def middle(got, twiddle):
     tables = [jnp.asarray(t) for t in (*lattice_tables(), *depth_tables())]
     return pl.pallas_call(
         middle_kernel,
         out_shape=jax.ShapeDtypeStruct((DEVICES * 32, 128), F32),
-        in_specs=[pl.BlockSpec(memory_space=pltpu.VMEM)] * 7,
+        in_specs=[pl.BlockSpec(memory_space=pltpu.VMEM)] * 6,
         out_specs=pl.BlockSpec(memory_space=pltpu.VMEM),
-        scratch_shapes=[pltpu.VMEM((NZ, SITES), BF16), pltpu.VMEM((NZ, SITES), BF16)],
+        scratch_shapes=[
+            pltpu.VMEM((NZ, SITES), BF16),
+            pltpu.VMEM((NZ, SITES), BF16),
+            pltpu.VMEM((2 * SLOTS * BRICK, 128), F32),
+            pltpu.VMEM((LAYERS, DEVICES, 128), F32),
+        ],
         compiler_params=pltpu.CompilerParams(vmem_limit_bytes=56 << 20),
         name="middle",
-    )(cells, places, twiddle, *tables)
-
-
-def final_kernel(pieces, lap_z, lap_x, lap_y, cell_high, cell_low, out_re, out_im, rows_ref):
+    )(got, twiddle, *tables)
+
+
+def final_kernel(pieces, lap_z, lap_x, lap_y, cell_high, cell_low, out_re, out_im):
     block = lax.broadcasted_iota(jnp.int32, (8, 128), 1) // 32
     scale = -1.0 / math.sqrt(PLANE * PLANE * NZ)
     outs = (out_re, out_im)
@@ -206,9 +243,7 @@
                     kx = (pair * 2 + h) * 4 + r
                     factor = scale / (along_z + lap_x[kx] + lap_y[t] + SCREEN)
                     for ri in range(2):
-                        rows_ref[pl.ds((ri * 4 + t) * 256 + kx, 8, stride=32), :] = (
-                            tiles[ri][r] * factor
-                        )
+                        outs[ri][pl.ds(kx * 8 + t * 2 + b, 8, stride=256), :] = tiles[ri][r] * factor
 
         @pl.when(pair == 0)
         def _():
@@ -221,14 +256,7 @@
                     line = jnp.where(block == j, moved, line)
                 for t in range(4):
                     factor = scale / (along_z[0:1] + 4.0 + lap_y[t, 0:1] + SCREEN)
-                    outs[ri][b, 256:257, t * 128 : t * 128 + 128] = line[t : t + 1] * factor
-
-        @pl.when(pair == 3)
-        def _():
-            for ri in range(2):
-                for t in range(4):
-                    at = (ri * 4 + t) * 256
-                    outs[ri][b, 0:256, t * 128 : t * 128 + 128] = rows_ref[at : at + 256, :]
+                    outs[ri][pl.ds(2048 + t * 2 + b, 1), :] = line[t : t + 1] * factor
 
         return 0
 
@@ -249,16 +277,18 @@
 def final(pieces, lap_z):
     lap_x, lap_y = lap_tables()
     tables = [jnp.asarray(t) for t in (lap_x, lap_y, *cell_tables())]
-    shape = jax.ShapeDtypeStruct((2, KX, PLANE), F32)
-    return pl.pallas_call(
+    shape = jax.ShapeDtypeStruct((KX * 8, 128), F32)
+    outs = pl.pallas_call(
         final_kernel,
         out_shape=(shape, shape),
         in_specs=[pl.BlockSpec(memory_space=pltpu.VMEM)] * 6,
         out_specs=(pl.BlockSpec(memory_space=pltpu.VMEM), pl.BlockSpec(memory_space=pltpu.VMEM)),
-        scratch_shapes=[pltpu.VMEM((8 * 256, 128), F32)],
         compiler_params=pltpu.CompilerParams(vmem_limit_bytes=56 << 20),
         name="final",
     )(pieces, lap_z, *tables)
+    return tuple(
+        o.reshape(KX, 4, 2, 128).transpose(2, 0, 1, 3).reshape(2, KX, PLANE) for o in outs
+    )
 
 
 def twiddle_of(device):
@@ -280,16 +310,11 @@
     device = lax.axis_index("zg") * 32 + lax.axis_index("zl")
     live = jnp.arange(CAP, dtype=jnp.int32)[None, :] < brick_live
     place = (brick_xy[0] * BLOCKS + brick_xy[1]).astype(F32).reshape(LAYERS, CAP)
-    place = jnp.where(live, place, -1.0).reshape(SLOTS, 1)
-    by_parity = jnp.swapaxes(brick_data.reshape(SLOTS, 8, 2, 256), 1, 2)
-    outgoing = jnp.concatenate(
-        [by_parity.reshape(SLOTS * BRICK, 256), jnp.broadcast_to(place, (SLOTS, 256))], axis=0
-    )
-    sent = outgoing.T.reshape(DEVICES, 1, SLOTS * (BRICK + 1))
-    got = lax.all_to_all(sent, AXES, 0, 0, tiled=True).reshape(DEVICES, SLOTS * (BRICK + 1))
-    cells = got[:, : SLOTS * BRICK].T
-    places = got[:, SLOTS * BRICK :].reshape(DEVICES, LAYERS, CAP).transpose(1, 0, 2)
-    rows = middle(cells, places, twiddle_of(device))
+    place = jnp.where(live, place, -1.0).reshape(1, SLOTS)
+    place = jnp.pad(place, ((0, 0), (0, 128 - SLOTS)))
+    sent = send(brick_data.reshape(SLOTS * BRICK, 256), place)
+    got = lax.all_to_all(sent.reshape(DEVICES, 1, CHUNK * 128), AXES, 0, 0, tiled=True)
+    rows = middle(got.reshape(DEVICES * CHUNK, 128), twiddle_of(device))
     pieces = lax.all_to_all(rows.reshape(DEVICES, 32, 128), AXES, 0, 0, tiled=True)
     return final(pieces.reshape(DEVICES * 32, 128), lap_z_of(device))
 

time: 211 us -> 202 us (0.957)
  local copies, waits for them, and re-layouts: 14.7 us -> 2.29 us
  Pallas kernels: 41.1 us -> 43.8 us
    pallas_call x2 -> x0, local copies, waits for them, and re-layouts: 4.89 us -> none  [final(): pl.pallas_call(final_kernel, out_shape=(shape, shape), in_specs=[pl.Block...]
    reshape x2 -> x0, local copies, waits for them, and re-layouts: 3.73 us -> none  [the longest x1 2.73 us: on_device(): sent = outgoing.T.reshape(DEVICES, 1, SLOTS * (BRICK + 1))]
    pallas_call x0 -> x1, Pallas kernels: none -> 2.59 us  [send(): pl.pallas_call(send_kernel, out_shape=jax.ShapeDtypeStruct((DEVICES * CHU...]
where the time goes in v2:
time: 202 us
  waiting for transfers between devices  129 us (64%)
  Pallas kernels  43.8 us (22%)
  starting transfers between devices  23.7 us (12%)
  other arithmetic  2.32 us (1%)
  local copies, waits for them, and re-layouts  2.29 us (1%)
    all_to_all x1, waiting for transfers between devices, on_device(): lax.all_to_all(rows.reshape(DEVICES, 32, 128), AXES, 0, 0, tiled=True)  96.6 us
    all_to_all x1, waiting for transfers between devices, on_device(): lax.all_to_all(sent.reshape(DEVICES, 1, CHUNK * 128), AXES, 0, 0, tiled=T...  32.5 us
    pallas_call x1, Pallas kernels, middle(): pl.pallas_call(middle_kernel, out_shape=jax.ShapeDtypeStruct((DEVICES * 3...  29.7 us
    all_to_all x1, starting transfers between devices, on_device(): lax.all_to_all(sent.reshape(DEVICES, 1, CHUNK * 128), AXES, 0, 0, tiled=T...  15.7 us
    pallas_call x1, Pallas kernels, final(): pl.pallas_call(final_kernel, out_shape=(shape, shape), in_specs=[pl.Block...  11.4 us
    all_to_all x1, starting transfers between devices, on_device(): lax.all_to_all(rows.reshape(DEVICES, 32, 128), AXES, 0, 0, tiled=True)  8.07 us
  transfers between devices with their start and end apart: 2, of which 2 were waited for; matrix products, arithmetic and copies ran while one was open for 0% of the time, Pallas kernels for 0%

profile of v2, /device:TPU:1, one launch (start us, length us, event | category | flops | bytes accessed | tf_op | source)
XLA Modules:
  0.0 201.8 jit_solution(6773487012341588151)
XLA Ops:
  0.6 0.7 iota_compare_fusion
  1.4 0.1 lt.45
  1.4 0.8 convert_select_fusion
  2.2 0.5 pad.4.place
  2.7 2.6 %send.1 = f32[2304,128]{1,0:T(8,128)} custom-call(f32[1024,256]{1,0:T(8,128)} %bitcast.19, f32[1,128]{1,0:T(1,128)} %pad.4.place), custom_call_target="tpu_custom_call" | custom-call | tf_op jit(solution)/shard_map/send/pallas_call | solution.py:109
  5.3 15.7 %all-to-all-start = ((f32[256,1,1152]{2,1,0:T(1,128)}), f32[256,1,1152]{2,1,0:T(1,128)S(1)}, u32[]{:S(2)}, u32[]{:S(2)}) async-start(f32[256,1,1152]{2,1,0:T(1,128)} %bitcast.18), calls=%async_computation | async-start | bytes 2359296 | tf_op jit(solution)/shard_map/all_to_all | solution.py:316
  21.0 0.2 sine_negate_fusion
  21.2 0.6 pad_maximum_fusion.twiddle
  21.8 32.5 %all-to-all-done = f32[256,1,1152]{2,1,0:T(1,128)S(1)} async-done(((f32[256,1,1152]{2,1,0:T(1,128)}), f32[256,1,1152]{2,1,0:T(1,128)S(1)}, u32[]{:S(2)}, u32[]{:S(2)}) %all-to-all-start) | async-done | bytes 1179680 | tf_op jit(solution)/shard_map/all_to_all | solution.py:316
  54.3 0.0 copy-start
  54.3 1.0 copy-done
  55.3 29.7 %middle.1 = f32[8192,128]{1,0:T(8,128)} custom-call(f32[2304,128]{1,0:T(8,128)} %bitcast.17, f32[2,1024]{1,0:T(2,128)} %pad_maximum_fusion.twiddle, bf16[1024,2048]{1,0:T(8,128)(2,1)} %constant.122.clone.lat_high, bf16[1024,2048]{1,0:T(8,128)(2,1)} %constant.123.clone.lat_low, bf16[2,512,512]{2,1,0:T(8,128)(2,1)} %constant.124.clone.dep_high, ...), custom_call_target="tpu_custom_call" | custom-call | tf_op jit(solution)/shard_map/middle/pallas_call | solution.py:198
  85.0 8.1 %all-to-all-start.1 = ((f32[256,32,128]{2,1,0:T(8,128)}), f32[256,32,128]{2,1,0:T(8,128)}, u32[]{:S(2)}, u32[]{:S(2)}) async-start(f32[256,32,128]{2,1,0:T(8,128)} %bitcast.16), calls=%async_computation.1 | async-start | bytes 8388608 | tf_op jit(solution)/shard_map/all_to_all | solution.py:318
  93.1 0.1 multiply_multiply_fusion
  93.2 96.6 %all-to-all-done.1 = f32[256,32,128]{2,1,0:T(8,128)} async-done(((f32[256,32,128]{2,1,0:T(8,128)}), f32[256,32,128]{2,1,0:T(8,128)}, u32[]{:S(2)}, u32[]{:S(2)}) %all-to-all-start.1) | async-done | bytes 4194336 | tf_op jit(solution)/shard_map/all_to_all | solution.py:318
  189.7 0.7 broadcast_in_dim.12.lap_z
  190.4 11.4 %final.1 = (f32[2056,128]{1,0:T(8,128)}, f32[2056,128]{1,0:T(8,128)}) custom-call(f32[8192,128]{1,0:T(8,128)} %bitcast.5.pieces, f32[2,8,128]{2,1,0:T(8,128)} %broadcast_in_dim.12.lap_z, f32[32,8,128]{2,1,0:T(8,128)} %constant.126.clone.lap_x, f32[4,8,128]{2,1,0:T(8,128)} %constant.127.clone.lap_y, bf16[320,512]{1,0:T(8,128)(2,1)} %constant.128.clone.cell_high, ...), custom_call_target="tpu_custom_call" | custom-call | tf_op jit(solution)/shard_map/final/pallas_call | solution.py:281
Async XLA Ops:
  5.3 48.9 %all-to-all-start = ((f32[256,1,1152]{2,1,0:T(1,128)}), f32[256,1,1152]{2,1,0:T(1,128)S(1)}, u32[]{:S(2)}, u32[]{:S(2)}) async-start(f32[256,1,1152]{2,1,0:T(1,128)} %bitcast.18), calls=%async_computation | async-start | bytes 2359296 | tf_op jit(solution)/shard_map/all_to_all | solution.py:316
  54.3 1.0 copy-start
  85.0 104.7 %all-to-all-start.1 = ((f32[256,32,128]{2,1,0:T(8,128)}), f32[256,32,128]{2,1,0:T(8,128)}, u32[]{:S(2)}, u32[]{:S(2)}) async-start(f32[256,32,128]{2,1,0:T(8,128)} %bitcast.16), calls=%async_computation.1 | async-start | bytes 8388608 | tf_op jit(solution)/shard_map/all_to_all | solution.py:318

commit v3 on v2

v3 whole, which is shorter than its diff:
```python
import math

import jax
import jax.numpy as jnp
import numpy as np
from jax import lax
from jax.experimental import pallas as pl
from jax.experimental.pallas import tpu as pltpu
from jax.sharding import PartitionSpec as P

AXES = ("zg", "zl")
NZ = 512
PLANE = 512
BRICK = 16
BLOCKS = 32
LAYERS = 4
CAP = 16
GROUPS = 8
DEVICES = 256
KX = 257
SLOTS = LAYERS * CAP
SITES = BLOCKS * BLOCKS
SCREEN = 0.25
TOGETHER = 4
CHUNK = 9
BF16 = jnp.bfloat16
F32 = jnp.float32


def reverse_bits(values, digits):
    result = values * 0
    for digit in range(digits):
        result = result | ((values >> digit) & 1) << (digits - 1 - digit)
    return result


def halves_np(table):
    high = table.astype(np.float32).astype(jnp.bfloat16)
    low = (table - high.astype(np.float64)).astype(np.float32).astype(jnp.bfloat16)
    return high, low


def lattice_tables():
    inner, by = np.divmod(np.arange(256), BLOCKS)
    k_high, ky = np.divmod(np.arange(256), BLOCKS)
    tables = []
    for k_low in range(4):
        turn = inner[:, None] * (k_low + 4 * k_high)[None, :] + by[:, None] * ky[None, :]
        angle = 2.0 * np.pi * (turn % BLOCKS) / BLOCKS
        real, imag = np.cos(angle), -np.sin(angle)
        if k_low == 1:
            below = [imag, -real]
        elif k_low == 3:
            below = [-imag, real]
        else:
            below = [0.0 * real, 0.0 * real]
        tables.append(np.block([[real, imag], below]))
    return halves_np(np.stack(tables))


def depth_tables():
    device = np.arange(DEVICES)
    kz = reverse_bits(2 * device, 9)
    q, g, zh = np.meshgrid(np.arange(LAYERS), np.arange(GROUPS), np.arange(8), indexing="ij")
    tables = []
    for parity in range(2):
        z = (g * 64 + q * 16 + 2 * zh + parity).reshape(-1)
        angle = 2.0 * np.pi * (kz[:, None] * z[None, :] % NZ) / NZ
        cos, sin = np.cos(angle), np.sin(angle)
        tables.append(np.block([[cos, sin], [-sin, cos]]))
    return halves_np(np.stack(tables))


def cell_tables():
    yy, xx = np.divmod(np.arange(DEVICES), BRICK)

    def block(k1y, k1x):
        angle = 2.0 * np.pi * ((k1y[:, None] * yy + k1x[:, None] * xx) % BRICK) / BRICK
        cos, sin = np.cos(angle), np.sin(angle)
        return np.block([[cos, sin], [-sin, cos]])

    t, j, k1x = (a.reshape(-1) for a in np.meshgrid(np.arange(4), np.arange(4), np.arange(8), indexing="ij"))
    main = block(4 * t + j, k1x)
    j, t = (a.reshape(-1) for a in np.meshgrid(np.arange(4), np.arange(8), indexing="ij"))
    last = block(4 * (t % 4) + j, np.full(32, 8))
    return halves_np(np.concatenate([main, last], axis=0))


def lap_tables():
    along_x = 4.0 * np.sin(np.pi * np.arange(288) / PLANE) ** 2
    along_y = 4.0 * np.sin(np.pi * np.arange(PLANE) / PLANE) ** 2
    rows = along_x[:256].reshape(8, 32).T
    lap_x = np.broadcast_to(rows[:, :, None], (32, 8, 128)).astype(np.float32)
    lap_y = np.broadcast_to(along_y.reshape(4, 1, 128), (4, 8, 128)).astype(np.float32)
    return lap_x, lap_y


def split(values):
    high = values.astype(BF16)
    return high, (values - high.astype(F32)).astype(BF16)


def dot(a, b):
    return jnp.dot(a, b, preferred_element_type=F32)


def dot3(a_high, a_low, b_high, b_low):
    return dot(a_high, b_high) + dot(a_high, b_low) + dot(a_low, b_high)


def send_kernel(bricks, xy, live, out):
    for h in range(2):
        for i in range(8):
            block = bricks[i * 128 : i * 128 + 128, h * 128 : h * 128 + 128]
            out[pl.ds(h * 128 * CHUNK + i, 128, stride=CHUNK), :] = block.T
    slot = lax.broadcasted_iota(jnp.int32, (1, SLOTS), 1)
    count = jnp.zeros((1, SLOTS), jnp.int32)
    for q in range(LAYERS):
        count = jnp.where(slot // CAP == q, live[0, q], count)
    place = jnp.where(slot % CAP < count, xy[0:1, :] * BLOCKS + xy[1:2, :], -1)
    place = jnp.concatenate([place, jnp.full((1, 128 - SLOTS), -1, jnp.int32)], axis=1)
    out[pl.ds(8, DEVICES, stride=CHUNK), :] = jnp.broadcast_to(place.astype(F32), (DEVICES, 128))


def send(bricks, xy, live):
    return pl.pallas_call(
        send_kernel,
        out_shape=jax.ShapeDtypeStruct((DEVICES * CHUNK, 128), F32),
        in_specs=[
            pl.BlockSpec(memory_space=pltpu.VMEM),
            pl.BlockSpec(memory_space=pltpu.VMEM),
            pl.BlockSpec(memory_space=pltpu.SMEM),
        ],
        out_specs=pl.BlockSpec(memory_space=pltpu.VMEM),
        compiler_params=pltpu.CompilerParams(vmem_limit_bytes=56 << 20),
        name="send",
    )(bricks, xy, live)


def read_cells(got, cells, places):
    for i in range(8):
        block = got[pl.ds(i, DEVICES, stride=CHUNK), :].T
        for h in range(2):
            at = h * 1024 + i * 128
            cells[at : at + 128, :] = block[:, h * 128 : h * 128 + 128]
    codes = got[pl.ds(8, DEVICES, stride=CHUNK), :]
    for q in range(LAYERS):
        places[q] = codes if q == 0 else pltpu.roll(codes, 128 - q * CAP, 1)


def spread_cells(cells, q, c, h, lane_group):
    tops, lows = [], []
    for parity in range(2):
        row = cells[pl.ds(h * 1024 + q * 256 + c * 16 + parity, 8, stride=2), :]
        tops.append(row.astype(BF16).astype(F32))
        lows.append(row - tops[-1])
    spread = [jnp.where(lane_group == g, piece, 0.0) for piece in tops + lows for g in range(4)]
    return jnp.concatenate(spread, axis=0).astype(BF16)


def place_layers(cells, places, field_high, field_low):
    lane_group = lax.broadcasted_iota(jnp.int32, (8, 128), 1) // 32
    site = lax.broadcasted_iota(jnp.int32, (128, SITES), 1).astype(F32)

    def place_layer(q, _):
        for h in range(2):
            where = places[q, h * 128 : h * 128 + 128, :]
            total = None
            for first in range(0, CAP, TOGETHER):
                slots = range(first, first + TOGETHER)
                spread = [spread_cells(cells, q, c, h, lane_group) for c in slots]
                chosen = [jnp.where(where[:, c : c + 1] == site, 1.0, 0.0).astype(BF16) for c in slots]
                part = dot(jnp.concatenate(spread, axis=1), jnp.concatenate(chosen, axis=0))
                total = part if total is None else total + part
            layer = total[:64] + total[64:]
            x = [layer[:, k * 256 : k * 256 + 256] for k in range(4)]
            even, odd = x[0] + x[2], x[1] + x[3]
            high, low = split(
                jnp.concatenate([even + odd, even - odd, x[0] - x[2], x[1] - x[3]], axis=1)
            )
            for parity in range(2):
                at = pl.multiple_of(parity * 256 + q * 64 + h * 32, 32)
                field_high[pl.ds(at, 32), :] = high[parity * 32 : parity * 32 + 32]
                field_low[pl.ds(at, 32), :] = low[parity * 32 : parity * 32 + 32]
        return 0

    lax.fori_loop(0, LAYERS, place_layer, 0)


def middle_kernel(
    got_any, twiddle, lat_high, lat_low, dep_any, out, got, dep, field_high, field_low, cells, places, spec, sems
):
    step = pl.program_id(0)

    @pl.when(step == 0)
    def _():
        fetch_dep = pltpu.make_async_copy(dep_any, dep, sems.at[1])
        fetch_dep.start()
        fetch_got = pltpu.make_async_copy(got_any, got, sems.at[0])
        fetch_got.start()
        fetch_got.wait()
        read_cells(got, cells, places)
        place_layers(cells, places, field_high, field_low)
        fetch_dep.wait()

    for even in range(2):
        @pl.when((step == 0) | (step == 2) if even else (step == 1) | (step == 3))
        def _(even=even):
            if even:
                at = pl.multiple_of(step * 128, 256)
                from_cols, rows = pl.ds(at, 256), slice(0, 256)
            else:
                from_cols, rows = pl.ds(512, 512), slice(0, 512)
            spec[...] = dot3(
                field_high[:, from_cols], field_low[:, from_cols], lat_high[0, rows, :], lat_low[0, rows, :]
            )

    turn_re = twiddle[0:1, :]
    turn_im = twiddle[1:2, :]
    real = spec[:, 0:256] * turn_re - spec[:, 256:512] * turn_im
    imag = spec[:, 0:256] * turn_im + spec[:, 256:512] * turn_re
    sums = []
    for parity in range(2):
        rows = slice(parity * 256, parity * 256 + 256)
        high, low = split(jnp.concatenate([real[rows], imag[rows]], axis=0))
        sums.append(dot3(dep[0, parity], dep[1, parity], high, low))
    flat = out.reshape(DEVICES * 8, 128)
    for b in range(2):
        both = sums[0] + sums[1] if b == 0 else sums[0] - sums[1]
        for ri in range(2):
            for h in range(2):
                flat[pl.ds((b * 2 + ri) * 2 + h, DEVICES, stride=8), :] = both[
                    ri * 256 : ri * 256 + 256, h * 128 : h * 128 + 128
                ]


def middle(got, twiddle):
    lat_high, lat_low = (jnp.asarray(t) for t in lattice_tables())
    dep = jnp.asarray(np.stack(depth_tables()))
    whole = pl.BlockSpec(memory_space=pl.ANY)
    quarter = pl.BlockSpec((1, 512, 512), lambda step: (step, 0, 0))
    return pl.pallas_call(
        middle_kernel,
        grid=(4,),
        out_shape=jax.ShapeDtypeStruct((DEVICES, 32, 128), F32),
        in_specs=[whole, pl.BlockSpec((2, 256), lambda step: (0, step)), quarter, quarter, whole],
        out_specs=pl.BlockSpec((DEVICES, 8, 128), lambda step: (0, step, 0)),
        scratch_shapes=[
            pltpu.VMEM((DEVICES * CHUNK, 128), F32),
            pltpu.VMEM(dep.shape, BF16),
            pltpu.VMEM((NZ, SITES), BF16),
            pltpu.VMEM((NZ, SITES), BF16),
            pltpu.VMEM((2 * SLOTS * BRICK, 128), F32),
            pltpu.VMEM((LAYERS, DEVICES, 128), F32),
            pltpu.VMEM((NZ, 512), F32),
            pltpu.SemaphoreType.DMA((2,)),
        ],
        compiler_params=pltpu.CompilerParams(vmem_limit_bytes=56 << 20),
        name="middle",
    )(got, twiddle, lat_high, lat_low, dep)


def final_kernel(pieces, lap_z, lap_x, lap_y, cell_high, cell_low, out_re, out_im):
    step = pl.program_id(0)
    block = lax.broadcasted_iota(jnp.int32, (8, 128), 1) // 32
    scale = -1.0 / math.sqrt(PLANE * PLANE * NZ)
    outs = (out_re, out_im)
    flat = pieces.reshape(DEVICES * 8, 128)
    for b in range(2):
        parts = []
        for ri in range(2):
            halves = [flat[pl.ds((b * 2 + ri) * 2 + h, DEVICES, stride=8), :] for h in range(2)]
            parts.append(jnp.concatenate(halves, axis=1))
        high, low = split(jnp.concatenate(parts, axis=0))
        result = dot3(cell_high[0:256, :], cell_low[0:256, :], high, low)
        along_z = lap_z[b]
        for h in range(2):
            along_x = [lap_x[step + 16 * h + 4 * r] + (along_z + SCREEN) for r in range(4)]
            for t in range(4):
                tiles = []
                for ri in range(2):
                    at = ri * 128 + t * 32
                    row = [
                        result[at + j * 8 : at + j * 8 + 8, h * 128 : h * 128 + 128]
                        for j in range(4)
                    ]
                    tiles.append(transpose_blocks(row, block))
                for r in range(4):
                    kx = step + 16 * h + 4 * r
                    factor = scale / (along_x[r] + lap_y[t])
                    for ri in range(2):
                        outs[ri][pl.ds(kx * 8 + t * 2 + b, 8, stride=256), :] = tiles[ri][r] * factor

        @pl.when(step == 0)
        def _():
            last = dot3(cell_high[256:320, :], cell_low[256:320, :], high[:, :128], low[:, :128])
            for ri in range(2):
                line = jnp.zeros((8, 128), F32)
                for j in range(4):
                    part = last[ri * 32 + j * 8 : ri * 32 + j * 8 + 8, :]
                    moved = part if j == 0 else pltpu.roll(part, 32 * j, 1)
                    line = jnp.where(block == j, moved, line)
                for t in range(4):
                    factor = scale / (along_z + 4.0 + lap_y[t, 0:1] + SCREEN)
                    outs[ri][2048 + t * 2 + b : 2049 + t * 2 + b, :] = line[t : t + 1] * factor


def transpose_blocks(row, block):
    tiles = []
    for r in range(4):
        tile = row[r]
        for j in range(4):
            if j != r:
                tile = jnp.where(block == j, pltpu.roll(row[j], (32 * (j - r)) % 128, 1), tile)
        tiles.append(tile)
    return tiles


def final(pieces, lap_z):
    lap_x, lap_y = lap_tables()
    tables = [jnp.asarray(t) for t in (lap_x, lap_y, *cell_tables())]
    shape = jax.ShapeDtypeStruct((KX * 8, 128), F32)
    vmem = pl.BlockSpec(memory_space=pltpu.VMEM)
    rows = pl.BlockSpec((KX * 8, 128), lambda step: (0, 0))
    outs = pl.pallas_call(
        final_kernel,
        grid=(4,),
        out_shape=(shape, shape),
        in_specs=[
            pl.BlockSpec((DEVICES, 8, 128), lambda step: (0, step, 0)),
            pl.BlockSpec(memory_space=pltpu.SMEM),
            vmem,
            vmem,
            vmem,
            vmem,
        ],
        out_specs=(rows, rows),
        compiler_params=pltpu.CompilerParams(vmem_limit_bytes=24 << 20),
        name="final",
    )(pieces, lap_z, *tables)
    return tuple(
        o.reshape(KX, 4, 2, 128).transpose(2, 0, 1, 3).reshape(2, KX, PLANE) for o in outs
    )


def twiddle_of(device):
    yy = device // BRICK
    xx = device % BRICK
    column = jnp.arange(SITES, dtype=jnp.int32)
    kx = column // 256 + 4 * (column % 256 // BLOCKS)
    turn = (kx * xx + (column % BLOCKS) * yy) % PLANE
    angle = (2.0 * math.pi / PLANE) * turn.astype(F32)
    return jnp.stack([jnp.cos(angle), -jnp.sin(angle)])


def lap_z_of(device):
    kz = reverse_bits(2 * device + jnp.arange(2, dtype=jnp.int32), 9)
    return 4.0 * jnp.sin(math.pi * kz.astype(F32) / NZ) ** 2


def on_device(brick_data, brick_xy, brick_live):
    device = lax.axis_index("zg") * 32 + lax.axis_index("zl")
    sent = send(brick_data.reshape(SLOTS * BRICK, 256), brick_xy, brick_live.T)
    got = lax.all_to_all(sent.reshape(DEVICES, 1, CHUNK * 128), AXES, 0, 0, tiled=True)
    rows = middle(got.reshape(DEVICES * CHUNK, 128), twiddle_of(device))
    pieces = lax.all_to_all(rows, AXES, 0, 0, tiled=True)
    return final(pieces, lap_z_of(device))


def solution(mesh):
    in_specs = (P(AXES, None, None), P(None, AXES), P(None, AXES))
    out_specs = (P(AXES, None, None), P(AXES, None, None))
    return jax.shard_map(
        on_device, mesh=mesh, in_specs=in_specs, out_specs=out_specs, check_vma=False
    )
```

time: 202 us -> 186 us (0.921)
  Pallas kernels: 43.8 us -> 29.9 us
    pallas_call x2, Pallas kernels: 41.2 us -> 27.3 us  [the longest x1 18 us: middle(): pl.pallas_call(middle_kernel, grid=(4,), out_shape=jax.ShapeDtypeStruct((...]
where the time goes in v3:
time: 186 us; the launch traced here: 185 us
  waiting for transfers between devices  129 us (69%)
  Pallas kernels  29.9 us (16%)
  starting transfers between devices  23.9 us (13%)
    all_to_all x1, waiting for transfers between devices, on_device(): pieces = lax.all_to_all(rows, AXES, 0, 0, tiled=True)  96.6 us
    all_to_all x1, waiting for transfers between devices, on_device(): lax.all_to_all(sent.reshape(DEVICES, 1, CHUNK * 128), AXES, 0, 0, tiled=T...  32.5 us
    pallas_call x1, Pallas kernels, middle(): pl.pallas_call(middle_kernel, grid=(4,), out_shape=jax.ShapeDtypeStruct((...  18 us
    all_to_all x1, starting transfers between devices, on_device(): lax.all_to_all(sent.reshape(DEVICES, 1, CHUNK * 128), AXES, 0, 0, tiled=T...  15.7 us
    pallas_call x1, Pallas kernels, final(): pl.pallas_call(final_kernel, grid=(4,), out_shape=(shape, shape), in_spec...  9.32 us
    all_to_all x1, starting transfers between devices, on_device(): pieces = lax.all_to_all(rows, AXES, 0, 0, tiled=True)  8.22 us
  transfers between devices with their start and end apart: 2, of which 2 were waited for; matrix products, arithmetic and copies ran while one was open for 0% of the time, Pallas kernels for 0%

profile of v3, /device:TPU:1, one launch (start us, length us, event | category | flops | bytes accessed | tf_op | source)
XLA Modules:
  0.0 185.5 jit_solution(7850553005060277252)
XLA Ops:
  0.6 2.6 %send.1 = f32[2304,128]{1,0:T(8,128)} custom-call(f32[1024,256]{1,0:T(8,128)} %bitcast.16, s32[2,64]{1,0:T(2,128)} %xy.1, s32[1,4]{1,0:T(1,128)} %bitcast.17), custom_call_target="tpu_custom_call" | custom-call | tf_op jit(solution)/shard_map/send/pallas_call | solution.py:126
  3.2 15.7 %all-to-all-start = ((f32[256,1,1152]{2,1,0:T(1,128)}), f32[256,1,1152]{2,1,0:T(1,128)S(1)}, u32[]{:S(2)}, u32[]{:S(2)}) async-start(f32[256,1,1152]{2,1,0:T(1,128)} %bitcast.15), calls=%async_computation | async-start | bytes 2359296 | tf_op jit(solution)/shard_map/all_to_all | solution.py:364
  18.9 0.2 sine_negate_fusion
  19.1 0.6 pad_maximum_fusion.twiddle
  19.7 32.5 %all-to-all-done = f32[256,1,1152]{2,1,0:T(1,128)S(1)} async-done(((f32[256,1,1152]{2,1,0:T(1,128)}), f32[256,1,1152]{2,1,0:T(1,128)S(1)}, u32[]{:S(2)}, u32[]{:S(2)}) %all-to-all-start) | async-done | bytes 1179680 | tf_op jit(solution)/shard_map/all_to_all | solution.py:364
  52.2 0.0 copy-start.4
  52.2 1.0 copy-done.4
  53.2 18.0 %middle.1 = f32[256,32,128]{2,1,0:T(8,128)} custom-call(f32[2304,128]{1,0:T(8,128)} %bitcast.14, f32[2,1024]{1,0:T(2,128)} %pad_maximum_fusion.twiddle, bf16[4,512,512]{2,1,0:T(8,128)(2,1)} %constant.135.clone.lat_high, bf16[4,512,512]{2,1,0:T(8,128)(2,1)} %constant.136.clone.lat_low, bf16[2,2,512,512]{3,2,1,0:T(8,128)(2,1)} %constant.137.clone.dep_any), custom_call_target="tpu_custom_call" | custom-call | tf_op jit(solution)/shard_map/middle/pallas_call | solution.py:242
  71.2 0.0 copy-start
  71.2 0.0 copy-start.1
  71.2 0.0 copy-start.2
  71.3 0.0 copy-start.3
  71.3 8.2 %all-to-all-start.1 = ((f32[256,32,128]{2,1,0:T(8,128)}), f32[256,32,128]{2,1,0:T(8,128)}, u32[]{:S(2)}, u32[]{:S(2)}) async-start(f32[256,32,128]{2,1,0:T(8,128)} %middle.1), calls=%async_computation.1 | async-start | bytes 8388608 | tf_op jit(solution)/shard_map/all_to_all | solution.py:366
  79.5 0.1 multiply_multiply_fusion.lap_z
  79.6 96.6 %all-to-all-done.1.pieces = f32[256,32,128]{2,1,0:T(8,128)} async-done(((f32[256,32,128]{2,1,0:T(8,128)}), f32[256,32,128]{2,1,0:T(8,128)}, u32[]{:S(2)}, u32[]{:S(2)}) %all-to-all-start.1) | async-done | bytes 4194336 | tf_op jit(solution)/shard_map/all_to_all | solution.py:366
  176.1 0.0 copy-done
  176.1 0.0 copy-done.1
  176.1 0.0 copy-done.2
  176.2 0.0 copy-done.3
  176.2 9.3 %final.1 = (f32[2056,128]{1,0:T(8,128)}, f32[2056,128]{1,0:T(8,128)}) custom-call(f32[256,32,128]{2,1,0:T(8,128)} %all-to-all-done.1.pieces, f32[2]{0:T(128)S(1)} %multiply_multiply_fusion.lap_z, f32[32,8,128]{2,1,0:T(8,128)S(1)} %copy-done.2, f32[4,8,128]{2,1,0:T(8,128)S(1)} %copy-done.3, bf16[320,512]{1,0:T(8,128)(2,1)S(1)} %copy-done.1, ...), custom_call_target="tpu_custom_call" | custom-call | tf_op jit(solution)/shard_map/final/pallas_call | solution.py:325
Async XLA Ops:
  3.2 48.9 %all-to-all-start = ((f32[256,1,1152]{2,1,0:T(1,128)}), f32[256,1,1152]{2,1,0:T(1,128)S(1)}, u32[]{:S(2)}, u32[]{:S(2)}) async-start(f32[256,1,1152]{2,1,0:T(1,128)} %bitcast.15), calls=%async_computation | async-start | bytes 2359296 | tf_op jit(solution)/shard_map/all_to_all | solution.py:364
  52.2 1.0 copy-start.4
  71.2 104.9 %copy-start = (bf16[320,512]{1,0:T(8,128)(2,1)S(1)}, bf16[320,512]{1,0:T(8,128)(2,1)}, u32[]{:S(2)}) copy-start(bf16[320,512]{1,0:T(8,128)(2,1)} %constant.141.clone.cell_low) | copy-start | bytes 983044
  71.2 104.9 %copy-start.1 = (bf16[320,512]{1,0:T(8,128)(2,1)S(1)}, bf16[320,512]{1,0:T(8,128)(2,1)}, u32[]{:S(2)}) copy-start(bf16[320,512]{1,0:T(8,128)(2,1)} %constant.140.clone.cell_high) | copy-start | bytes 983044
  71.2 104.9 %copy-start.2 = (f32[32,8,128]{2,1,0:T(8,128)S(1)}, f32[32,8,128]{2,1,0:T(8,128)}, u32[]{:S(2)}) copy-start(f32[32,8,128]{2,1,0:T(8,128)} %constant.138.clone.lap_x) | copy-start | bytes 393220
  71.3 104.9 %copy-start.3 = (f32[4,8,128]{2,1,0:T(8,128)S(1)}, f32[4,8,128]{2,1,0:T(8,128)}, u32[]{:S(2)}) copy-start(f32[4,8,128]{2,1,0:T(8,128)} %constant.139.clone.lap_y) | copy-start | bytes 49156
  71.3 104.9 %all-to-all-start.1 = ((f32[256,32,128]{2,1,0:T(8,128)}), f32[256,32,128]{2,1,0:T(8,128)}, u32[]{:S(2)}, u32[]{:S(2)}) async-start(f32[256,32,128]{2,1,0:T(8,128)} %middle.1), calls=%async_computation.1 | async-start | bytes 8388608 | tf_op jit(solution)/shard_map/all_to_all | solution.py:366

commit v4 on v3

--- a/solution.py
+++ b/solution.py
@@ -21,6 +21,7 @@
 SLOTS = LAYERS * CAP
 SITES = BLOCKS * BLOCKS
 SCREEN = 0.25
+FETCHED = 2
 TOGETHER = 4
 CHUNK = 9
 BF16 = jnp.bfloat16
@@ -184,115 +185,130 @@
                 field_low[pl.ds(at, 32), :] = low[parity * 32 : parity * 32 + 32]
         return 0
 
-    lax.fori_loop(0, LAYERS, place_layer, 0)
+    lax.fori_loop(0, LAYERS, place_layer, 0, unroll=True)
 
 
 def middle_kernel(
-    got_any, twiddle, lat_high, lat_low, dep_any, out, got, dep, field_high, field_low, cells, places, spec, sems
+    got_any, twiddle, lat_any, dep_any, out_any,
+    got, lat, dep, field_high, field_low, cells, places, out, sems,
 ):
-    step = pl.program_id(0)
-
-    @pl.when(step == 0)
-    def _():
-        fetch_dep = pltpu.make_async_copy(dep_any, dep, sems.at[1])
-        fetch_dep.start()
-        fetch_got = pltpu.make_async_copy(got_any, got, sems.at[0])
-        fetch_got.start()
-        fetch_got.wait()
-        read_cells(got, cells, places)
-        place_layers(cells, places, field_high, field_low)
-        fetch_dep.wait()
-
-    for even in range(2):
-        @pl.when((step == 0) | (step == 2) if even else (step == 1) | (step == 3))
-        def _(even=even):
-            if even:
-                at = pl.multiple_of(step * 128, 256)
-                from_cols, rows = pl.ds(at, 256), slice(0, 256)
-            else:
-                from_cols, rows = pl.ds(512, 512), slice(0, 512)
-            spec[...] = dot3(
-                field_high[:, from_cols], field_low[:, from_cols], lat_high[0, rows, :], lat_low[0, rows, :]
-            )
-
-    turn_re = twiddle[0:1, :]
-    turn_im = twiddle[1:2, :]
-    real = spec[:, 0:256] * turn_re - spec[:, 256:512] * turn_im
-    imag = spec[:, 0:256] * turn_im + spec[:, 256:512] * turn_re
-    sums = []
-    for parity in range(2):
-        rows = slice(parity * 256, parity * 256 + 256)
-        high, low = split(jnp.concatenate([real[rows], imag[rows]], axis=0))
-        sums.append(dot3(dep[0, parity], dep[1, parity], high, low))
-    flat = out.reshape(DEVICES * 8, 128)
-    for b in range(2):
-        both = sums[0] + sums[1] if b == 0 else sums[0] - sums[1]
-        for ri in range(2):
-            for h in range(2):
-                flat[pl.ds((b * 2 + ri) * 2 + h, DEVICES, stride=8), :] = both[
-                    ri * 256 : ri * 256 + 256, h * 128 : h * 128 + 128
-                ]
+    fetch_got = pltpu.make_async_copy(got_any, got, sems.at[0])
+    fetch_got.start()
+    fetch_dep = pltpu.make_async_copy(dep_any, dep, sems.at[1])
+    fetch_dep.start()
+    fetch_lat = [pltpu.make_async_copy(lat_any.at[k], lat.at[k], sems.at[2 + k]) for k in range(4)]
+    for fetch in fetch_lat:
+        fetch.start()
+    fetch_got.wait()
+    read_cells(got, cells, places)
+    place_layers(cells, places, field_high, field_low)
+    fetch_dep.wait()
+    leave = []
+    for k in range(4):
+        fetch_lat[k].wait()
+        cols = slice(512, 1024) if k % 2 else slice(k * 128, k * 128 + 256)
+        used = slice(0, 512) if k % 2 else slice(0, 256)
+        found = dot3(field_high[:, cols], field_low[:, cols], lat[k, 0, used, :], lat[k, 1, used, :])
+        turn_re = twiddle[0:1, k * 256 : k * 256 + 256]
+        turn_im = twiddle[1:2, k * 256 : k * 256 + 256]
+        real = found[:, 0:256] * turn_re - found[:, 256:512] * turn_im
+        imag = found[:, 0:256] * turn_im + found[:, 256:512] * turn_re
+        sums = []
+        for parity in range(2):
+            rows = slice(parity * 256, parity * 256 + 256)
+            high, low = split(jnp.concatenate([real[rows], imag[rows]], axis=0))
+            sums.append(dot3(dep[0, parity], dep[1, parity], high, low))
+        flat = out.at[k].reshape(DEVICES * 8, 128)
+        for b in range(2):
+            both = sums[0] + sums[1] if b == 0 else sums[0] - sums[1]
+            for ri in range(2):
+                for h in range(2):
+                    flat[pl.ds((b * 2 + ri) * 2 + h, DEVICES, stride=8), :] = both[
+                        ri * 256 : ri * 256 + 256, h * 128 : h * 128 + 128
+                    ]
+        leave.append(
+            pltpu.make_async_copy(out.at[k], out_any.at[:, k * 8 : k * 8 + 8, :], sems.at[6 + k])
+        )
+        leave[k].start()
+    for copy in leave:
+        copy.wait()
 
 
 def middle(got, twiddle):
-    lat_high, lat_low = (jnp.asarray(t) for t in lattice_tables())
+    lat = jnp.asarray(np.stack(lattice_tables(), axis=1))
     dep = jnp.asarray(np.stack(depth_tables()))
-    whole = pl.BlockSpec(memory_space=pl.ANY)
-    quarter = pl.BlockSpec((1, 512, 512), lambda step: (step, 0, 0))
+    hbm = pl.BlockSpec(memory_space=pltpu.HBM)
     return pl.pallas_call(
         middle_kernel,
-        grid=(4,),
         out_shape=jax.ShapeDtypeStruct((DEVICES, 32, 128), F32),
-        in_specs=[whole, pl.BlockSpec((2, 256), lambda step: (0, step)), quarter, quarter, whole],
-        out_specs=pl.BlockSpec((DEVICES, 8, 128), lambda step: (0, step, 0)),
+        in_specs=[
+            pl.BlockSpec(memory_space=pl.ANY),
+            pl.BlockSpec(memory_space=pltpu.VMEM),
+            hbm,
+            hbm,
+        ],
+        out_specs=hbm,
         scratch_shapes=[
             pltpu.VMEM((DEVICES * CHUNK, 128), F32),
+            pltpu.VMEM(lat.shape, BF16),
             pltpu.VMEM(dep.shape, BF16),
             pltpu.VMEM((NZ, SITES), BF16),
             pltpu.VMEM((NZ, SITES), BF16),
             pltpu.VMEM((2 * SLOTS * BRICK, 128), F32),
             pltpu.VMEM((LAYERS, DEVICES, 128), F32),
-            pltpu.VMEM((NZ, 512), F32),
-            pltpu.SemaphoreType.DMA((2,)),
+            pltpu.VMEM((4, DEVICES, 8, 128), F32),
+            pltpu.SemaphoreType.DMA((10,)),
         ],
-        compiler_params=pltpu.CompilerParams(vmem_limit_bytes=56 << 20),
+        compiler_params=pltpu.CompilerParams(vmem_limit_bytes=50 << 20),
         name="middle",
-    )(got, twiddle, lat_high, lat_low, dep)
-
-
-def final_kernel(pieces, lap_z, lap_x, lap_y, cell_high, cell_low, out_re, out_im):
-    step = pl.program_id(0)
+    )(got, twiddle, lat, dep)
+
+
+def final_kernel(
+    pieces_any, lap_z, lap_x, lap_y, cell_high, cell_low, out_re, out_im, pieces, sems
+):
     block = lax.broadcasted_iota(jnp.int32, (8, 128), 1) // 32
     scale = -1.0 / math.sqrt(PLANE * PLANE * NZ)
     outs = (out_re, out_im)
-    flat = pieces.reshape(DEVICES * 8, 128)
-    for b in range(2):
-        parts = []
-        for ri in range(2):
-            halves = [flat[pl.ds((b * 2 + ri) * 2 + h, DEVICES, stride=8), :] for h in range(2)]
-            parts.append(jnp.concatenate(halves, axis=1))
-        high, low = split(jnp.concatenate(parts, axis=0))
-        result = dot3(cell_high[0:256, :], cell_low[0:256, :], high, low)
-        along_z = lap_z[b]
-        for h in range(2):
-            along_x = [lap_x[step + 16 * h + 4 * r] + (along_z + SCREEN) for r in range(4)]
-            for t in range(4):
-                tiles = []
-                for ri in range(2):
-                    at = ri * 128 + t * 32
-                    row = [
-                        result[at + j * 8 : at + j * 8 + 8, h * 128 : h * 128 + 128]
-                        for j in range(4)
-                    ]
-                    tiles.append(transpose_blocks(row, block))
-                for r in range(4):
-                    kx = step + 16 * h + 4 * r
-                    factor = scale / (along_x[r] + lap_y[t])
+    fetches = [
+        pltpu.make_async_copy(pieces_any.at[:, k * 8 : k * 8 + 8, :], pieces.at[k], sems.at[k])
+        for k in range(4)
+    ]
+    for fetch in fetches:
+        fetch.start()
+    for k in range(4):
+        if k % FETCHED == 0:
+            for fetch in fetches[k : k + FETCHED]:
+                fetch.wait()
+        flat = pieces.at[k].reshape(DEVICES * 8, 128)
+        for b in range(2):
+            parts = []
+            for ri in range(2):
+                halves = [flat[pl.ds((b * 2 + ri) * 2 + h, DEVICES, stride=8), :] for h in range(2)]
+                parts.append(jnp.concatenate(halves, axis=1))
+            high, low = split(jnp.concatenate(parts, axis=0))
+            result = dot3(cell_high[0:256, :], cell_low[0:256, :], high, low)
+            along_z = lap_z[b]
+            for h in range(2):
+                along_x = [lap_x[k + 16 * h + 4 * r] + (along_z + SCREEN) for r in range(4)]
+                for t in range(4):
+                    tiles = []
                     for ri in range(2):
-                        outs[ri][pl.ds(kx * 8 + t * 2 + b, 8, stride=256), :] = tiles[ri][r] * factor
-
-        @pl.when(step == 0)
-        def _():
+                        at = ri * 128 + t * 32
+                        row = [
+                            result[at + j * 8 : at + j * 8 + 8, h * 128 : h * 128 + 128]
+                            for j in range(4)
+                        ]
+                        tiles.append(transpose_blocks(row, block))
+                    for r in range(4):
+                        kx = k + 16 * h + 4 * r
+                        factor = scale / (along_x[r] + lap_y[t])
+                        for ri in range(2):
+                            outs[ri][pl.ds(kx * 8 + t * 2 + b, 8, stride=256), :] = (
+                                tiles[ri][r] * factor
+                            )
+            if k > 0:
+                continue
             last = dot3(cell_high[256:320, :], cell_low[256:320, :], high[:, :128], low[:, :128])
             for ri in range(2):
                 line = jnp.zeros((8, 128), F32)
@@ -306,13 +322,13 @@
 
 
 def transpose_blocks(row, block):
+    low, even = block < 2, block % 2 == 0
+    first = [jnp.where(low, row[j], pltpu.roll(row[j + 2], 64, 1)) for j in range(2)]
+    last = [jnp.where(low, pltpu.roll(row[j], 64, 1), row[j + 2]) for j in range(2)]
     tiles = []
-    for r in range(4):
-        tile = row[r]
-        for j in range(4):
-            if j != r:
-                tile = jnp.where(block == j, pltpu.roll(row[j], (32 * (j - r)) % 128, 1), tile)
-        tiles.append(tile)
+    for a, b in (first, last):
+        tiles.append(jnp.where(even, a, pltpu.roll(b, 32, 1)))
+        tiles.append(jnp.where(even, pltpu.roll(a, 96, 1), b))
     return tiles
 
 
@@ -321,20 +337,16 @@
     tables = [jnp.asarray(t) for t in (lap_x, lap_y, *cell_tables())]
     shape = jax.ShapeDtypeStruct((KX * 8, 128), F32)
     vmem = pl.BlockSpec(memory_space=pltpu.VMEM)
-    rows = pl.BlockSpec((KX * 8, 128), lambda step: (0, 0))
     outs = pl.pallas_call(
         final_kernel,
-        grid=(4,),
         out_shape=(shape, shape),
         in_specs=[
-            pl.BlockSpec((DEVICES, 8, 128), lambda step: (0, step, 0)),
+            pl.BlockSpec(memory_space=pl.ANY),
             pl.BlockSpec(memory_space=pltpu.SMEM),
-            vmem,
-            vmem,
-            vmem,
-            vmem,
+            *[vmem] * 4,
         ],
-        out_specs=(rows, rows),
+        out_specs=(vmem, vmem),
+        scratch_shapes=[pltpu.VMEM((4, DEVICES, 8, 128), F32), pltpu.SemaphoreType.DMA((4,))],
         compiler_params=pltpu.CompilerParams(vmem_limit_bytes=24 << 20),
         name="final",
     )(pieces, lap_z, *tables)

time: 186 us -> 179 us (0.962)
  Pallas kernels: 29.9 us -> 24.5 us
    pallas_call x2, Pallas kernels: 27.3 us -> 21.7 us  [the longest x1 14.1 us: middle(): pl.pallas_call(middle_kernel, out_shape=jax.ShapeDtypeStruct((DEVICES, 32...]
where the time goes in v4:
time: 179 us
  waiting for transfers between devices  130 us (73%)
  Pallas kernels  24.5 us (14%)
  starting transfers between devices  23.9 us (13%)
    all_to_all x1, waiting for transfers between devices, on_device(): pieces = lax.all_to_all(rows, AXES, 0, 0, tiled=True)  96.6 us
    all_to_all x1, waiting for transfers between devices, on_device(): lax.all_to_all(sent.reshape(DEVICES, 1, CHUNK * 128), AXES, 0, 0, tiled=T...  33.1 us
    all_to_all x1, starting transfers between devices, on_device(): lax.all_to_all(sent.reshape(DEVICES, 1, CHUNK * 128), AXES, 0, 0, tiled=T...  15.7 us
    pallas_call x1, Pallas kernels, middle(): pl.pallas_call(middle_kernel, out_shape=jax.ShapeDtypeStruct((DEVICES, 32...  14.1 us
    all_to_all x1, starting transfers between devices, on_device(): pieces = lax.all_to_all(rows, AXES, 0, 0, tiled=True)  8.24 us
    pallas_call x1, Pallas kernels, final(): pl.pallas_call(final_kernel, out_shape=(shape, shape), in_specs=[pl.Block...  7.61 us
  transfers between devices with their start and end apart: 2, of which 2 were waited for; matrix products, arithmetic and copies ran while one was open for 0% of the time, Pallas kernels for 0%

profile of v4, /device:TPU:1, one launch (start us, length us, event | category | flops | bytes accessed | tf_op | source)
XLA Modules:
  0.0 179.2 jit_solution(6077897540542603555)
XLA Ops:
  0.6 0.0 copy-start
  0.6 2.7 %send.1 = f32[2304,128]{1,0:T(8,128)} custom-call(f32[1024,256]{1,0:T(8,128)} %bitcast.16, s32[2,64]{1,0:T(2,128)} %xy.1, s32[1,4]{1,0:T(1,128)} %bitcast.17), custom_call_target="tpu_custom_call" | custom-call | tf_op jit(solution)/shard_map/send/pallas_call | solution.py:127
  3.4 15.7 %all-to-all-start = ((f32[256,1,1152]{2,1,0:T(1,128)}), f32[256,1,1152]{2,1,0:T(1,128)S(1)}, u32[]{:S(2)}, u32[]{:S(2)}) async-start(f32[256,1,1152]{2,1,0:T(1,128)} %bitcast.15), calls=%async_computation | async-start | bytes 2359296 | tf_op jit(solution)/shard_map/all_to_all | solution.py:376
  19.1 0.2 sine_negate_fusion
  19.3 33.1 %all-to-all-done = f32[256,1,1152]{2,1,0:T(1,128)S(1)} async-done(((f32[256,1,1152]{2,1,0:T(1,128)}), f32[256,1,1152]{2,1,0:T(1,128)S(1)}, u32[]{:S(2)}, u32[]{:S(2)}) %all-to-all-start) | async-done | bytes 1179680 | tf_op jit(solution)/shard_map/all_to_all | solution.py:376
  52.3 0.0 copy-done
  52.3 14.1 %middle.1 = f32[256,32,128]{2,1,0:T(8,128)} custom-call(f32[2304,128]{1,0:T(8,128)S(1)} %bitcast.14, f32[2,1024]{1,0:T(2,128)S(1)} %pad_maximum_fusion.twiddle, bf16[4,2,512,512]{3,2,1,0:T(8,128)(2,1)} %constant.133.clone.lat_any, bf16[2,2,512,512]{3,2,1,0:T(8,128)(2,1)S(1)} %copy-done), custom_call_target="tpu_custom_call" | custom-call | tf_op jit(solution)/shard_map/middle/pallas_call | solution.py:241
  66.5 0.0 copy-start.1
  66.5 0.0 copy-start.2
  66.5 0.0 copy-start.3
  66.5 0.0 copy-start.4
  66.5 8.2 %all-to-all-start.1 = ((f32[256,32,128]{2,1,0:T(8,128)}), f32[256,32,128]{2,1,0:T(8,128)}, u32[]{:S(2)}, u32[]{:S(2)}) async-start(f32[256,32,128]{2,1,0:T(8,128)} %middle.1), calls=%async_computation.1 | async-start | bytes 8388608 | tf_op jit(solution)/shard_map/all_to_all | solution.py:378
  74.8 0.1 multiply_multiply_fusion.lap_z
  74.8 96.6 %all-to-all-done.1.pieces_any = f32[256,32,128]{2,1,0:T(8,128)} async-done(((f32[256,32,128]{2,1,0:T(8,128)}), f32[256,32,128]{2,1,0:T(8,128)}, u32[]{:S(2)}, u32[]{:S(2)}) %all-to-all-start.1) | async-done | bytes 4194336 | tf_op jit(solution)/shard_map/all_to_all | solution.py:378
  171.4 0.0 copy-done.1
  171.4 0.0 copy-done.2
  171.4 0.0 copy-done.3
  171.4 0.0 copy-done.4
  171.4 7.6 %final.1 = (f32[2056,128]{1,0:T(8,128)}, f32[2056,128]{1,0:T(8,128)}) custom-call(f32[256,32,128]{2,1,0:T(8,128)} %all-to-all-done.1.pieces_any, f32[2]{0:T(128)S(1)} %multiply_multiply_fusion.lap_z, f32[32,8,128]{2,1,0:T(8,128)S(1)} %copy-done.3, f32[4,8,128]{2,1,0:T(8,128)S(1)} %copy-done.4, bf16[320,512]{1,0:T(8,128)(2,1)S(1)} %copy-done.2, ...), custom_call_target="tpu_custom_call" | custom-call | tf_op jit(solution)/shard_map/final/pallas_call | solution.py:340
  (1 shorter events, 0.0 us)
Async XLA Ops:
  0.6 51.7 %copy-start = (bf16[2,2,512,512]{3,2,1,0:T(8,128)(2,1)S(1)}, bf16[2,2,512,512]{3,2,1,0:T(8,128)(2,1)}, u32[]{:S(2)}) copy-start(bf16[2,2,512,512]{3,2,1,0:T(8,128)(2,1)} %constant.134.clone.dep_any) | copy-start | bytes 6291460
  3.4 48.9 %all-to-all-start = ((f32[256,1,1152]{2,1,0:T(1,128)}), f32[256,1,1152]{2,1,0:T(1,128)S(1)}, u32[]{:S(2)}, u32[]{:S(2)}) async-start(f32[256,1,1152]{2,1,0:T(1,128)} %bitcast.15), calls=%async_computation | async-start | bytes 2359296 | tf_op jit(solution)/shard_map/all_to_all | solution.py:376
  66.5 104.9 %copy-start.1 = (bf16[320,512]{1,0:T(8,128)(2,1)S(1)}, bf16[320,512]{1,0:T(8,128)(2,1)}, u32[]{:S(2)}) copy-start(bf16[320,512]{1,0:T(8,128)(2,1)} %constant.138.clone.cell_low) | copy-start | bytes 983044
  66.5 104.9 %copy-start.2 = (bf16[320,512]{1,0:T(8,128)(2,1)S(1)}, bf16[320,512]{1,0:T(8,128)(2,1)}, u32[]{:S(2)}) copy-start(bf16[320,512]{1,0:T(8,128)(2,1)} %constant.137.clone.cell_high) | copy-start | bytes 983044
  66.5 104.9 %copy-start.3 = (f32[32,8,128]{2,1,0:T(8,128)S(1)}, f32[32,8,128]{2,1,0:T(8,128)}, u32[]{:S(2)}) copy-start(f32[32,8,128]{2,1,0:T(8,128)} %constant.135.clone.lap_x) | copy-start | bytes 393220
  66.5 104.9 %copy-start.4 = (f32[4,8,128]{2,1,0:T(8,128)S(1)}, f32[4,8,128]{2,1,0:T(8,128)}, u32[]{:S(2)}) copy-start(f32[4,8,128]{2,1,0:T(8,128)} %constant.136.clone.lap_y) | copy-start | bytes 49156
  66.5 104.9 %all-to-all-start.1 = ((f32[256,32,128]{2,1,0:T(8,128)}), f32[256,32,128]{2,1,0:T(8,128)}, u32[]{:S(2)}, u32[]{:S(2)}) async-start(f32[256,32,128]{2,1,0:T(8,128)} %middle.1), calls=%async_computation.1 | async-start | bytes 8388608 | tf_op jit(solution)/shard_map/all_to_all | solution.py:378

commit v5 on v4

--- a/solution.py
+++ b/solution.py
@@ -61,30 +61,35 @@
 
 def depth_tables():
     device = np.arange(DEVICES)
-    kz = reverse_bits(2 * device, 9)
-    q, g, zh = np.meshgrid(np.arange(LAYERS), np.arange(GROUPS), np.arange(8), indexing="ij")
+    kz_all = reverse_bits(2 * device, 9)
+    q, g, zh = np.meshgrid(np.arange(LAYERS), np.arange(4), np.arange(8), indexing="ij")
     tables = []
     for parity in range(2):
-        z = (g * 64 + q * 16 + 2 * zh + parity).reshape(-1)
-        angle = 2.0 * np.pi * (kz[:, None] * z[None, :] % NZ) / NZ
-        cos, sin = np.cos(angle), np.sin(angle)
-        tables.append(np.block([[cos, sin], [-sin, cos]]))
+        for half in range(2):
+            kz = kz_all[half * 128 : half * 128 + 128]
+            z = (g * 64 + q * 16 + 2 * zh + parity).reshape(-1)
+            angle = 2.0 * np.pi * (kz[:, None] * z[None, :] % NZ) / NZ
+            cos, sin = np.cos(angle), np.sin(angle)
+            tables.append(np.block([[cos, sin], [-sin, cos]]))
     return halves_np(np.stack(tables))
 
 
 def cell_tables():
-    yy, xx = np.divmod(np.arange(DEVICES), BRICK)
+    yy, xx = np.divmod(np.arange(128), BRICK)
 
     def block(k1y, k1x):
         angle = 2.0 * np.pi * ((k1y[:, None] * yy + k1x[:, None] * xx) % BRICK) / BRICK
         cos, sin = np.cos(angle), np.sin(angle)
         return np.block([[cos, sin], [-sin, cos]])
 
-    t, j, k1x = (a.reshape(-1) for a in np.meshgrid(np.arange(4), np.arange(4), np.arange(8), indexing="ij"))
-    main = block(4 * t + j, k1x)
-    j, t = (a.reshape(-1) for a in np.meshgrid(np.arange(4), np.arange(8), indexing="ij"))
-    last = block(4 * (t % 4) + j, np.full(32, 8))
-    return halves_np(np.concatenate([main, last], axis=0))
+    tables = []
+    for odd in range(2):
+        t, j, k1x = (a.reshape(-1) for a in np.meshgrid(np.arange(4), np.arange(2), np.arange(8), indexing="ij"))
+        main = block(4 * t + 2 * j + odd, k1x)
+        j, t = (a.reshape(-1) for a in np.meshgrid(np.arange(2), np.arange(8), indexing="ij"))
+        last = block(4 * (t % 4) + 2 * j + odd, np.full(16, 8))
+        tables.append(np.concatenate([main, last], axis=0))
+    return halves_np(np.stack(tables))
 
 
 def lap_tables():
@@ -164,6 +169,7 @@
     site = lax.broadcasted_iota(jnp.int32, (128, SITES), 1).astype(F32)
 
     def place_layer(q, _):
+        layers = []
         for h in range(2):
             where = places[q, h * 128 : h * 128 + 128, :]
             total = None
@@ -173,14 +179,15 @@
                 chosen = [jnp.where(where[:, c : c + 1] == site, 1.0, 0.0).astype(BF16) for c in slots]
                 part = dot(jnp.concatenate(spread, axis=1), jnp.concatenate(chosen, axis=0))
                 total = part if total is None else total + part
-            layer = total[:64] + total[64:]
+            layers.append(total[:64] + total[64:])
+        for half, layer in enumerate((layers[0] + layers[1], layers[0] - layers[1])):
             x = [layer[:, k * 256 : k * 256 + 256] for k in range(4)]
             even, odd = x[0] + x[2], x[1] + x[3]
             high, low = split(
                 jnp.concatenate([even + odd, even - odd, x[0] - x[2], x[1] - x[3]], axis=1)
             )
             for parity in range(2):
-                at = pl.multiple_of(parity * 256 + q * 64 + h * 32, 32)
+                at = pl.multiple_of(parity * 256 + half * 128 + q * 32, 32)
                 field_high[pl.ds(at, 32), :] = high[parity * 32 : parity * 32 + 32]
                 field_low[pl.ds(at, 32), :] = low[parity * 32 : parity * 32 + 32]
         return 0
@@ -213,19 +220,22 @@
         turn_im = twiddle[1:2, k * 256 : k * 256 + 256]
         real = found[:, 0:256] * turn_re - found[:, 256:512] * turn_im
         imag = found[:, 0:256] * turn_im + found[:, 256:512] * turn_re
-        sums = []
-        for parity in range(2):
-            rows = slice(parity * 256, parity * 256 + 256)
-            high, low = split(jnp.concatenate([real[rows], imag[rows]], axis=0))
-            sums.append(dot3(dep[0, parity], dep[1, parity], high, low))
         flat = out.at[k].reshape(DEVICES * 8, 128)
-        for b in range(2):
-            both = sums[0] + sums[1] if b == 0 else sums[0] - sums[1]
-            for ri in range(2):
-                for h in range(2):
-                    flat[pl.ds((b * 2 + ri) * 2 + h, DEVICES, stride=8), :] = both[
-                        ri * 256 : ri * 256 + 256, h * 128 : h * 128 + 128
-                    ]
+        for half in range(2):
+            sums = []
+            for parity in range(2):
+                rows = slice(parity * 256 + half * 128, parity * 256 + half * 128 + 128)
+                high, low = split(jnp.concatenate([real[rows], imag[rows]], axis=0))
+                at = parity * 2 + half
+                sums.append(dot3(dep[0, at], dep[1, at], high, low))
+            for b in range(2):
+                both = sums[0] + sums[1] if b == 0 else sums[0] - sums[1]
+                for ri in range(2):
+                    for h in range(2):
+                        at = half * 128 * 8 + (b * 2 + ri) * 2 + h
+                        flat[pl.ds(at, 128, stride=8), :] = both[
+                            ri * 128 : ri * 128 + 128, h * 128 : h * 128 + 128
+                        ]
         leave.append(
             pltpu.make_async_copy(out.at[k], out_any.at[:, k * 8 : k * 8 + 8, :], sems.at[6 + k])
         )
@@ -282,21 +292,29 @@
                 fetch.wait()
         flat = pieces.at[k].reshape(DEVICES * 8, 128)
         for b in range(2):
-            parts = []
-            for ri in range(2):
-                halves = [flat[pl.ds((b * 2 + ri) * 2 + h, DEVICES, stride=8), :] for h in range(2)]
-                parts.append(jnp.concatenate(halves, axis=1))
-            high, low = split(jnp.concatenate(parts, axis=0))
-            result = dot3(cell_high[0:256, :], cell_low[0:256, :], high, low)
+            sides = []
+            for side in range(2):
+                parts = []
+                for ri in range(2):
+                    at = side * 128 * 8 + (b * 2 + ri) * 2
+                    parts.append([flat[pl.ds(at + h, 128, stride=8), :] for h in range(2)])
+                sides.append(jnp.concatenate([jnp.concatenate(p, axis=1) for p in parts], axis=0))
+            folded = [split(sides[0] + sides[1]), split(sides[0] - sides[1])]
+            results = [
+                dot3(cell_high[odd, 0:128, :], cell_low[odd, 0:128, :], *folded[odd])
+                for odd in range(2)
+            ]
             along_z = lap_z[b]
             for h in range(2):
                 along_x = [lap_x[k + 16 * h + 4 * r] + (along_z + SCREEN) for r in range(4)]
                 for t in range(4):
                     tiles = []
                     for ri in range(2):
-                        at = ri * 128 + t * 32
+                        at = ri * 64 + t * 16
                         row = [
-                            result[at + j * 8 : at + j * 8 + 8, h * 128 : h * 128 + 128]
+                            results[j % 2][
+                                at + j // 2 * 8 : at + j // 2 * 8 + 8, h * 128 : h * 128 + 128
+                            ]
                             for j in range(4)
                         ]
                         tiles.append(transpose_blocks(row, block))
@@ -309,11 +327,17 @@
                             )
             if k > 0:
                 continue
-            last = dot3(cell_high[256:320, :], cell_low[256:320, :], high[:, :128], low[:, :128])
+            lasts = [
+                dot3(
+                    cell_high[odd, 128:160, :], cell_low[odd, 128:160, :], folded[odd][0][:, :128], folded[odd][1][:, :128]
+                )
+                for odd in range(2)
+            ]
             for ri in range(2):
                 line = jnp.zeros((8, 128), F32)
                 for j in range(4):
-                    part = last[ri * 32 + j * 8 : ri * 32 + j * 8 + 8, :]
+                    at = ri * 16 + j // 2 * 8
+                    part = lasts[j % 2][at : at + 8, :]
                     moved = part if j == 0 else pltpu.roll(part, 32 * j, 1)
                     line = jnp.where(block == j, moved, line)
                 for t in range(4):

time: 179 us -> 178 us (level)
  Pallas kernels: 24.5 us -> 22.4 us
where the time goes in v5:
time: 178 us; the launch traced here: 177 us
  waiting for transfers between devices  130 us (73%)
  starting transfers between devices  24.1 us (14%)
  Pallas kernels  22.4 us (13%)
    all_to_all x1, waiting for transfers between devices, on_device(): pieces = lax.all_to_all(rows, AXES, 0, 0, tiled=True)  96.6 us
    all_to_all x1, waiting for transfers between devices, on_device(): lax.all_to_all(sent.reshape(DEVICES, 1, CHUNK * 128), AXES, 0, 0, tiled=T...  33.1 us
    all_to_all x1, starting transfers between devices, on_device(): lax.all_to_all(sent.reshape(DEVICES, 1, CHUNK * 128), AXES, 0, 0, tiled=T...  15.7 us
    pallas_call x1, Pallas kernels, middle(): pl.pallas_call(middle_kernel, out_shape=jax.ShapeDtypeStruct((DEVICES, 32...  12.6 us
    all_to_all x1, starting transfers between devices, on_device(): pieces = lax.all_to_all(rows, AXES, 0, 0, tiled=True)  8.41 us
    pallas_call x1, Pallas kernels, final(): pl.pallas_call(final_kernel, out_shape=(shape, shape), in_specs=[pl.Block...  7.23 us
  transfers between devices with their start and end apart: 2, of which 2 were waited for; matrix products, arithmetic and copies ran while one was open for 0% of the time, Pallas kernels for 0%

profile of v5, /device:TPU:1, one launch (start us, length us, event | category | flops | bytes accessed | tf_op | source)
XLA Modules:
  0.0 177.3 jit_solution(5631497591429399583)
XLA Ops:
  0.6 2.6 %send.1 = f32[2304,128]{1,0:T(8,128)} custom-call(f32[1024,256]{1,0:T(8,128)} %bitcast.16, s32[2,64]{1,0:T(2,128)} %xy.1, s32[1,4]{1,0:T(1,128)} %bitcast.17), custom_call_target="tpu_custom_call" | custom-call | tf_op jit(solution)/shard_map/send/pallas_call | solution.py:132
  3.2 0.0 copy-start
  3.2 15.7 %all-to-all-start = ((f32[256,1,1152]{2,1,0:T(1,128)}), f32[256,1,1152]{2,1,0:T(1,128)S(1)}, u32[]{:S(2)}, u32[]{:S(2)}) async-start(f32[256,1,1152]{2,1,0:T(1,128)} %bitcast.15), calls=%async_computation | async-start | bytes 2359296 | tf_op jit(solution)/shard_map/all_to_all | solution.py:400
  18.9 0.2 sine_negate_fusion
  19.1 33.1 %all-to-all-done = f32[256,1,1152]{2,1,0:T(1,128)S(1)} async-done(((f32[256,1,1152]{2,1,0:T(1,128)}), f32[256,1,1152]{2,1,0:T(1,128)S(1)}, u32[]{:S(2)}, u32[]{:S(2)}) %all-to-all-start) | async-done | bytes 1179680 | tf_op jit(solution)/shard_map/all_to_all | solution.py:400
  52.2 0.0 copy-done
  52.2 12.6 %middle.1 = f32[256,32,128]{2,1,0:T(8,128)} custom-call(f32[2304,128]{1,0:T(8,128)S(1)} %bitcast.14, f32[2,1024]{1,0:T(2,128)S(1)} %pad_maximum_fusion.twiddle, bf16[4,2,512,512]{3,2,1,0:T(8,128)(2,1)} %constant.133.clone.lat_any, bf16[2,4,256,256]{3,2,1,0:T(8,128)(2,1)S(1)} %copy-done), custom_call_target="tpu_custom_call" | custom-call | tf_op jit(solution)/shard_map/middle/pallas_call | solution.py:251
  64.8 0.0 copy-start.1
  64.8 0.0 copy-start.2
  64.8 0.0 copy-start.3
  64.8 0.0 copy-start.4
  64.8 8.4 %all-to-all-start.1 = ((f32[256,32,128]{2,1,0:T(8,128)}), f32[256,32,128]{2,1,0:T(8,128)}, u32[]{:S(2)}, u32[]{:S(2)}) async-start(f32[256,32,128]{2,1,0:T(8,128)} %middle.1), calls=%async_computation.1 | async-start | bytes 8388608 | tf_op jit(solution)/shard_map/all_to_all | solution.py:402
  73.2 0.1 multiply_multiply_fusion.lap_z
  73.3 96.6 %all-to-all-done.1.pieces_any = f32[256,32,128]{2,1,0:T(8,128)} async-done(((f32[256,32,128]{2,1,0:T(8,128)}), f32[256,32,128]{2,1,0:T(8,128)}, u32[]{:S(2)}, u32[]{:S(2)}) %all-to-all-start.1) | async-done | bytes 4194336 | tf_op jit(solution)/shard_map/all_to_all | solution.py:402
  169.9 0.0 copy-done.1
  169.9 0.0 copy-done.2
  169.9 0.0 copy-done.3
  169.9 0.0 copy-done.4
  169.9 7.2 %final.1 = (f32[2056,128]{1,0:T(8,128)}, f32[2056,128]{1,0:T(8,128)}) custom-call(f32[256,32,128]{2,1,0:T(8,128)} %all-to-all-done.1.pieces_any, f32[2]{0:T(128)S(1)} %multiply_multiply_fusion.lap_z, f32[32,8,128]{2,1,0:T(8,128)S(1)} %copy-done.3, f32[4,8,128]{2,1,0:T(8,128)S(1)} %copy-done.4, bf16[2,160,256]{2,1,0:T(8,128)(2,1)S(1)} %copy-done.2, ...), custom_call_target="tpu_custom_call" | custom-call | tf_op jit(solution)/shard_map/final/pallas_call | solution.py:364
  (1 shorter events, 0.0 us)
Async XLA Ops:
  3.2 48.9 %copy-start = (bf16[2,4,256,256]{3,2,1,0:T(8,128)(2,1)S(1)}, bf16[2,4,256,256]{3,2,1,0:T(8,128)(2,1)}, u32[]{:S(2)}) copy-start(bf16[2,4,256,256]{3,2,1,0:T(8,128)(2,1)} %constant.134.clone.dep_any) | copy-start | bytes 3145732
  3.2 48.9 %all-to-all-start = ((f32[256,1,1152]{2,1,0:T(1,128)}), f32[256,1,1152]{2,1,0:T(1,128)S(1)}, u32[]{:S(2)}, u32[]{:S(2)}) async-start(f32[256,1,1152]{2,1,0:T(1,128)} %bitcast.15), calls=%async_computation | async-start | bytes 2359296 | tf_op jit(solution)/shard_map/all_to_all | solution.py:400
  64.8 105.1 %copy-start.1 = (bf16[2,160,256]{2,1,0:T(8,128)(2,1)S(1)}, bf16[2,160,256]{2,1,0:T(8,128)(2,1)}, u32[]{:S(2)}) copy-start(bf16[2,160,256]{2,1,0:T(8,128)(2,1)} %constant.138.clone.cell_low) | copy-start | bytes 491524
  64.8 105.1 %copy-start.2 = (bf16[2,160,256]{2,1,0:T(8,128)(2,1)S(1)}, bf16[2,160,256]{2,1,0:T(8,128)(2,1)}, u32[]{:S(2)}) copy-start(bf16[2,160,256]{2,1,0:T(8,128)(2,1)} %constant.137.clone.cell_high) | copy-start | bytes 491524
  64.8 105.1 %copy-start.3 = (f32[32,8,128]{2,1,0:T(8,128)S(1)}, f32[32,8,128]{2,1,0:T(8,128)}, u32[]{:S(2)}) copy-start(f32[32,8,128]{2,1,0:T(8,128)} %constant.135.clone.lap_x) | copy-start | bytes 393220
  64.8 105.1 %copy-start.4 = (f32[4,8,128]{2,1,0:T(8,128)S(1)}, f32[4,8,128]{2,1,0:T(8,128)}, u32[]{:S(2)}) copy-start(f32[4,8,128]{2,1,0:T(8,128)} %constant.136.clone.lap_y) | copy-start | bytes 49156
  64.8 105.1 %all-to-all-start.1 = ((f32[256,32,128]{2,1,0:T(8,128)}), f32[256,32,128]{2,1,0:T(8,128)}, u32[]{:S(2)}, u32[]{:S(2)}) async-start(f32[256,32,128]{2,1,0:T(8,128)} %middle.1), calls=%async_computation.1 | async-start | bytes 8388608 | tf_op jit(solution)/shard_map/all_to_all | solution.py:402

commit v6 on v5

--- a/solution.py
+++ b/solution.py
@@ -209,13 +209,20 @@
     fetch_got.wait()
     read_cells(got, cells, places)
     place_layers(cells, places, field_high, field_low)
-    fetch_dep.wait()
+    for fetch in (fetch_dep, *fetch_lat):
+        fetch.wait()
     leave = []
-    for k in range(4):
-        fetch_lat[k].wait()
+
+    def lattice(k):
         cols = slice(512, 1024) if k % 2 else slice(k * 128, k * 128 + 256)
         used = slice(0, 512) if k % 2 else slice(0, 256)
-        found = dot3(field_high[:, cols], field_low[:, cols], lat[k, 0, used, :], lat[k, 1, used, :])
+        return dot3(field_high[:, cols], field_low[:, cols], lat[k, 0, used, :], lat[k, 1, used, :])
+
+    ahead = lattice(0)
+    for k in range(4):
+        found = ahead
+        if k < 3:
+            ahead = lattice(k + 1)
         turn_re = twiddle[0:1, k * 256 : k * 256 + 256]
         turn_im = twiddle[1:2, k * 256 : k * 256 + 256]
         real = found[:, 0:256] * turn_re - found[:, 256:512] * turn_im

time: 178 us -> 177 us (level)
  no operation moved by 1% of the time
where the time goes in v6:
time: 177 us; the launch traced here: 176 us
  waiting for transfers between devices  130 us (73%)
  starting transfers between devices  24.1 us (14%)
  Pallas kernels  21.4 us (12%)
    all_to_all x1, waiting for transfers between devices, on_device(): pieces = lax.all_to_all(rows, AXES, 0, 0, tiled=True)  96.6 us
    all_to_all x1, waiting for transfers between devices, on_device(): lax.all_to_all(sent.reshape(DEVICES, 1, CHUNK * 128), AXES, 0, 0, tiled=T...  33.1 us
    all_to_all x1, starting transfers between devices, on_device(): lax.all_to_all(sent.reshape(DEVICES, 1, CHUNK * 128), AXES, 0, 0, tiled=T...  15.7 us
    pallas_call x1, Pallas kernels, middle(): pl.pallas_call(middle_kernel, out_shape=jax.ShapeDtypeStruct((DEVICES, 32...  11.5 us
    all_to_all x1, starting transfers between devices, on_device(): pieces = lax.all_to_all(rows, AXES, 0, 0, tiled=True)  8.41 us
    pallas_call x1, Pallas kernels, final(): pl.pallas_call(final_kernel, out_shape=(shape, shape), in_specs=[pl.Block...  7.23 us
  transfers between devices with their start and end apart: 2, of which 2 were waited for; matrix products, arithmetic and copies ran while one was open for 0% of the time, Pallas kernels for 0%

profile of v6, /device:TPU:1, one launch (start us, length us, event | category | flops | bytes accessed | tf_op | source)
XLA Modules:
  0.0 176.2 jit_solution(14981694589985948353)
XLA Ops:
  0.6 2.6 %send.1 = f32[2304,128]{1,0:T(8,128)} custom-call(f32[1024,256]{1,0:T(8,128)} %bitcast.16, s32[2,64]{1,0:T(2,128)} %xy.1, s32[1,4]{1,0:T(1,128)} %bitcast.17), custom_call_target="tpu_custom_call" | custom-call | tf_op jit(solution)/shard_map/send/pallas_call | solution.py:132
  3.2 0.0 copy-start
  3.2 15.7 %all-to-all-start = ((f32[256,1,1152]{2,1,0:T(1,128)}), f32[256,1,1152]{2,1,0:T(1,128)S(1)}, u32[]{:S(2)}, u32[]{:S(2)}) async-start(f32[256,1,1152]{2,1,0:T(1,128)} %bitcast.15), calls=%async_computation | async-start | bytes 2359296 | tf_op jit(solution)/shard_map/all_to_all | solution.py:407
  18.9 0.2 sine_negate_fusion
  19.1 33.1 %all-to-all-done = f32[256,1,1152]{2,1,0:T(1,128)S(1)} async-done(((f32[256,1,1152]{2,1,0:T(1,128)}), f32[256,1,1152]{2,1,0:T(1,128)S(1)}, u32[]{:S(2)}, u32[]{:S(2)}) %all-to-all-start) | async-done | bytes 1179680 | tf_op jit(solution)/shard_map/all_to_all | solution.py:407
  52.2 0.0 copy-done
  52.2 11.5 %middle.1 = f32[256,32,128]{2,1,0:T(8,128)} custom-call(f32[2304,128]{1,0:T(8,128)S(1)} %bitcast.14, f32[2,1024]{1,0:T(2,128)S(1)} %pad_maximum_fusion.twiddle, bf16[4,2,512,512]{3,2,1,0:T(8,128)(2,1)} %constant.133.clone.lat_any, bf16[2,4,256,256]{3,2,1,0:T(8,128)(2,1)S(1)} %copy-done), custom_call_target="tpu_custom_call" | custom-call | tf_op jit(solution)/shard_map/middle/pallas_call | solution.py:258
  63.7 0.0 copy-start.1
  63.7 0.0 copy-start.2
  63.7 0.0 copy-start.3
  63.8 0.0 copy-start.4
  63.8 8.4 %all-to-all-start.1 = ((f32[256,32,128]{2,1,0:T(8,128)}), f32[256,32,128]{2,1,0:T(8,128)}, u32[]{:S(2)}, u32[]{:S(2)}) async-start(f32[256,32,128]{2,1,0:T(8,128)} %middle.1), calls=%async_computation.1 | async-start | bytes 8388608 | tf_op jit(solution)/shard_map/all_to_all | solution.py:409
  72.2 0.1 multiply_multiply_fusion.lap_z
  72.2 96.6 %all-to-all-done.1.pieces_any = f32[256,32,128]{2,1,0:T(8,128)} async-done(((f32[256,32,128]{2,1,0:T(8,128)}), f32[256,32,128]{2,1,0:T(8,128)}, u32[]{:S(2)}, u32[]{:S(2)}) %all-to-all-start.1) | async-done | bytes 4194336 | tf_op jit(solution)/shard_map/all_to_all | solution.py:409
  168.8 0.0 copy-done.1
  168.8 0.0 copy-done.2
  168.8 0.0 copy-done.3
  168.8 0.0 copy-done.4
  168.8 7.2 %final.1 = (f32[2056,128]{1,0:T(8,128)}, f32[2056,128]{1,0:T(8,128)}) custom-call(f32[256,32,128]{2,1,0:T(8,128)} %all-to-all-done.1.pieces_any, f32[2]{0:T(128)S(1)} %multiply_multiply_fusion.lap_z, f32[32,8,128]{2,1,0:T(8,128)S(1)} %copy-done.3, f32[4,8,128]{2,1,0:T(8,128)S(1)} %copy-done.4, bf16[2,160,256]{2,1,0:T(8,128)(2,1)S(1)} %copy-done.2, ...), custom_call_target="tpu_custom_call" | custom-call | tf_op jit(solution)/shard_map/final/pallas_call | solution.py:371
  (1 shorter events, 0.0 us)
Async XLA Ops:
  3.2 48.9 %copy-start = (bf16[2,4,256,256]{3,2,1,0:T(8,128)(2,1)S(1)}, bf16[2,4,256,256]{3,2,1,0:T(8,128)(2,1)}, u32[]{:S(2)}) copy-start(bf16[2,4,256,256]{3,2,1,0:T(8,128)(2,1)} %constant.134.clone.dep_any) | copy-start | bytes 3145732
  3.2 48.9 %all-to-all-start = ((f32[256,1,1152]{2,1,0:T(1,128)}), f32[256,1,1152]{2,1,0:T(1,128)S(1)}, u32[]{:S(2)}, u32[]{:S(2)}) async-start(f32[256,1,1152]{2,1,0:T(1,128)} %bitcast.15), calls=%async_computation | async-start | bytes 2359296 | tf_op jit(solution)/shard_map/all_to_all | solution.py:407
  63.7 105.1 %copy-start.1 = (bf16[2,160,256]{2,1,0:T(8,128)(2,1)S(1)}, bf16[2,160,256]{2,1,0:T(8,128)(2,1)}, u32[]{:S(2)}) copy-start(bf16[2,160,256]{2,1,0:T(8,128)(2,1)} %constant.138.clone.cell_low) | copy-start | bytes 491524
  63.7 105.1 %copy-start.2 = (bf16[2,160,256]{2,1,0:T(8,128)(2,1)S(1)}, bf16[2,160,256]{2,1,0:T(8,128)(2,1)}, u32[]{:S(2)}) copy-start(bf16[2,160,256]{2,1,0:T(8,128)(2,1)} %constant.137.clone.cell_high) | copy-start | bytes 491524
  63.7 105.1 %copy-start.3 = (f32[32,8,128]{2,1,0:T(8,128)S(1)}, f32[32,8,128]{2,1,0:T(8,128)}, u32[]{:S(2)}) copy-start(f32[32,8,128]{2,1,0:T(8,128)} %constant.135.clone.lap_x) | copy-start | bytes 393220
  63.8 105.1 %copy-start.4 = (f32[4,8,128]{2,1,0:T(8,128)S(1)}, f32[4,8,128]{2,1,0:T(8,128)}, u32[]{:S(2)}) copy-start(f32[4,8,128]{2,1,0:T(8,128)} %constant.136.clone.lap_y) | copy-start | bytes 49156
  63.8 105.1 %all-to-all-start.1 = ((f32[256,32,128]{2,1,0:T(8,128)}), f32[256,32,128]{2,1,0:T(8,128)}, u32[]{:S(2)}, u32[]{:S(2)}) async-start(f32[256,32,128]{2,1,0:T(8,128)} %middle.1), calls=%async_computation.1 | async-start | bytes 8388608 | tf_op jit(solution)/shard_map/all_to_all | solution.py:409

commit v7 on v6

--- a/solution.py
+++ b/solution.py
@@ -21,7 +21,7 @@
 SLOTS = LAYERS * CAP
 SITES = BLOCKS * BLOCKS
 SCREEN = 0.25
-FETCHED = 2
+PITCH = 264
 TOGETHER = 4
 CHUNK = 9
 BF16 = jnp.bfloat16
@@ -115,29 +115,28 @@
 
 
 def send_kernel(bricks, xy, live, out):
-    for h in range(2):
-        for i in range(8):
-            block = bricks[i * 128 : i * 128 + 128, h * 128 : h * 128 + 128]
-            out[pl.ds(h * 128 * CHUNK + i, 128, stride=CHUNK), :] = block.T
+    for i in range(8):
+        out[pl.ds(i, 128, stride=CHUNK), :] = bricks[i * 128 : i * 128 + 128, :].T
     slot = lax.broadcasted_iota(jnp.int32, (1, SLOTS), 1)
     count = jnp.zeros((1, SLOTS), jnp.int32)
     for q in range(LAYERS):
         count = jnp.where(slot // CAP == q, live[0, q], count)
     place = jnp.where(slot % CAP < count, xy[0:1, :] * BLOCKS + xy[1:2, :], -1)
     place = jnp.concatenate([place, jnp.full((1, 128 - SLOTS), -1, jnp.int32)], axis=1)
-    out[pl.ds(8, DEVICES, stride=CHUNK), :] = jnp.broadcast_to(place.astype(F32), (DEVICES, 128))
+    out[pl.ds(8, 128, stride=CHUNK), :] = jnp.broadcast_to(place.astype(F32), (128, 128))
 
 
 def send(bricks, xy, live):
     return pl.pallas_call(
         send_kernel,
+        grid=(2,),
         out_shape=jax.ShapeDtypeStruct((DEVICES * CHUNK, 128), F32),
         in_specs=[
-            pl.BlockSpec(memory_space=pltpu.VMEM),
+            pl.BlockSpec((SLOTS * BRICK, 128), lambda h: (0, h)),
             pl.BlockSpec(memory_space=pltpu.VMEM),
             pl.BlockSpec(memory_space=pltpu.SMEM),
         ],
-        out_specs=pl.BlockSpec(memory_space=pltpu.VMEM),
+        out_specs=pl.BlockSpec((128 * CHUNK, 128), lambda h: (h, 0)),
         compiler_params=pltpu.CompilerParams(vmem_limit_bytes=56 << 20),
         name="send",
     )(bricks, xy, live)
@@ -282,7 +281,7 @@
 
 
 def final_kernel(
-    pieces_any, lap_z, lap_x, lap_y, cell_high, cell_low, out_re, out_im, pieces, sems
+    pieces_any, lap_z, lap_x, lap_y, cell_high, cell_low, out_re, out_im, pieces, held, sems
 ):
     block = lax.broadcasted_iota(jnp.int32, (8, 128), 1) // 32
     scale = -1.0 / math.sqrt(PLANE * PLANE * NZ)
@@ -294,8 +293,8 @@
     for fetch in fetches:
         fetch.start()
     for k in range(4):
-        if k % FETCHED == 0:
-            for fetch in fetches[k : k + FETCHED]:
+        if k < 2:
+            for fetch in fetches[:1] if k == 0 else fetches[1:]:
                 fetch.wait()
         flat = pieces.at[k].reshape(DEVICES * 8, 128)
         for b in range(2):
@@ -329,7 +328,7 @@
                         kx = k + 16 * h + 4 * r
                         factor = scale / (along_x[r] + lap_y[t])
                         for ri in range(2):
-                            outs[ri][pl.ds(kx * 8 + t * 2 + b, 8, stride=256), :] = (
+                            held[ri, pl.ds(kx * 8 + t * 2 + b, 8, stride=PITCH), :] = (
                                 tiles[ri][r] * factor
                             )
             if k > 0:
@@ -349,7 +348,20 @@
                     line = jnp.where(block == j, moved, line)
                 for t in range(4):
                     factor = scale / (along_z + 4.0 + lap_y[t, 0:1] + SCREEN)
-                    outs[ri][2048 + t * 2 + b : 2049 + t * 2 + b, :] = line[t : t + 1] * factor
+                    at = 8 * PITCH + t * 2 + b
+                    held[ri, at : at + 1, :] = line[t : t + 1] * factor
+
+    leave = []
+    for ri in range(2):
+        for k1x in range(9):
+            count = 256 if k1x < 8 else 8
+            kept = held.at[ri, pl.ds(k1x * PITCH, count), :]
+            leave.append(
+                pltpu.make_async_copy(kept, outs[ri].at[pl.ds(k1x * 256, count), :], sems.at[4 + ri * 9 + k1x])
+            )
+            leave[-1].start()
+    for copy in leave:
+        copy.wait()
 
 
 def transpose_blocks(row, block):
@@ -376,8 +388,12 @@
             pl.BlockSpec(memory_space=pltpu.SMEM),
             *[vmem] * 4,
         ],
-        out_specs=(vmem, vmem),
-        scratch_shapes=[pltpu.VMEM((4, DEVICES, 8, 128), F32), pltpu.SemaphoreType.DMA((4,))],
+        out_specs=(pl.BlockSpec(memory_space=pltpu.HBM), pl.BlockSpec(memory_space=pltpu.HBM)),
+        scratch_shapes=[
+            pltpu.VMEM((4, DEVICES, 8, 128), F32),
+            pltpu.VMEM((2, 8 * PITCH + 8, 128), F32),
+            pltpu.SemaphoreType.DMA((22,)),
+        ],
         compiler_params=pltpu.CompilerParams(vmem_limit_bytes=24 << 20),
         name="final",
     )(pieces, lap_z, *tables)

time: 177 us -> 175 us (0.989)
  no operation moved by 1% of the time
where the time goes in v7:
time: 175 us; the launch traced here: 174 us
  waiting for transfers between devices  130 us (74%)
  starting transfers between devices  23.9 us (14%)
  Pallas kernels  19.7 us (11%)
    all_to_all x1, waiting for transfers between devices, on_device(): pieces = lax.all_to_all(rows, AXES, 0, 0, tiled=True)  96.6 us
    all_to_all x1, waiting for transfers between devices, on_device(): lax.all_to_all(sent.reshape(DEVICES, 1, CHUNK * 128), AXES, 0, 0, tiled=T...  33.1 us
    all_to_all x1, starting transfers between devices, on_device(): lax.all_to_all(sent.reshape(DEVICES, 1, CHUNK * 128), AXES, 0, 0, tiled=T...  15.7 us
    pallas_call x1, Pallas kernels, middle(): pl.pallas_call(middle_kernel, out_shape=jax.ShapeDtypeStruct((DEVICES, 32...  11.5 us
    all_to_all x1, starting transfers between devices, on_device(): pieces = lax.all_to_all(rows, AXES, 0, 0, tiled=True)  8.24 us
    pallas_call x1, Pallas kernels, final(): pl.pallas_call(final_kernel, out_shape=(shape, shape), in_specs=[pl.Block...  5.88 us
  transfers between devices with their start and end apart: 2, of which 2 were waited for; matrix products, arithmetic and copies ran while one was open for 0% of the time, Pallas kernels for 0%

profile of v7, /device:TPU:1, one launch (start us, length us, event | category | flops | bytes accessed | tf_op | source)
XLA Modules:
  0.0 174.4 jit_solution(5380498451439127903)
XLA Ops:
  0.6 2.3 %send.1 = f32[2304,128]{1,0:T(8,128)} custom-call(f32[1024,256]{1,0:T(8,128)} %bitcast.16, s32[2,64]{1,0:T(2,128)} %xy.1, s32[1,4]{1,0:T(1,128)} %bitcast.17), custom_call_target="tpu_custom_call" | custom-call | tf_op jit(solution)/shard_map/send/pallas_call | solution.py:130
  2.9 0.0 copy-start
  3.0 15.7 %all-to-all-start = ((f32[256,1,1152]{2,1,0:T(1,128)}), f32[256,1,1152]{2,1,0:T(1,128)S(1)}, u32[]{:S(2)}, u32[]{:S(2)}) async-start(f32[256,1,1152]{2,1,0:T(1,128)} %bitcast.15), calls=%async_computation | async-start | bytes 2359296 | tf_op jit(solution)/shard_map/all_to_all | solution.py:423
  18.6 0.2 sine_negate_fusion
  18.8 33.1 %all-to-all-done = f32[256,1,1152]{2,1,0:T(1,128)S(1)} async-done(((f32[256,1,1152]{2,1,0:T(1,128)}), f32[256,1,1152]{2,1,0:T(1,128)S(1)}, u32[]{:S(2)}, u32[]{:S(2)}) %all-to-all-start) | async-done | bytes 1179680 | tf_op jit(solution)/shard_map/all_to_all | solution.py:423
  51.9 0.0 copy-done
  51.9 11.5 %middle.1 = f32[256,32,128]{2,1,0:T(8,128)} custom-call(f32[2304,128]{1,0:T(8,128)S(1)} %bitcast.14, f32[2,1024]{1,0:T(2,128)S(1)} %pad_maximum_fusion.twiddle, bf16[4,2,512,512]{3,2,1,0:T(8,128)(2,1)} %constant.133.clone.lat_any, bf16[2,4,256,256]{3,2,1,0:T(8,128)(2,1)S(1)} %copy-done), custom_call_target="tpu_custom_call" | custom-call | tf_op jit(solution)/shard_map/middle/pallas_call | solution.py:257
  63.4 0.0 copy-start.1
  63.4 0.0 copy-start.2
  63.4 0.0 copy-start.3
  63.5 0.0 copy-start.4
  63.5 8.2 %all-to-all-start.1 = ((f32[256,32,128]{2,1,0:T(8,128)}), f32[256,32,128]{2,1,0:T(8,128)}, u32[]{:S(2)}, u32[]{:S(2)}) async-start(f32[256,32,128]{2,1,0:T(8,128)} %middle.1), calls=%async_computation.1 | async-start | bytes 8388608 | tf_op jit(solution)/shard_map/all_to_all | solution.py:425
  71.7 0.1 multiply_multiply_fusion.lap_z
  71.8 96.6 %all-to-all-done.1.pieces_any = f32[256,32,128]{2,1,0:T(8,128)} async-done(((f32[256,32,128]{2,1,0:T(8,128)}), f32[256,32,128]{2,1,0:T(8,128)}, u32[]{:S(2)}, u32[]{:S(2)}) %all-to-all-start.1) | async-done | bytes 4194336 | tf_op jit(solution)/shard_map/all_to_all | solution.py:425
  168.4 0.0 copy-done.1
  168.4 0.0 copy-done.2
  168.4 0.0 copy-done.3
  168.4 0.0 copy-done.4
  168.4 5.9 %final.1 = (f32[2056,128]{1,0:T(8,128)}, f32[2056,128]{1,0:T(8,128)}) custom-call(f32[256,32,128]{2,1,0:T(8,128)} %all-to-all-done.1.pieces_any, f32[2]{0:T(128)S(1)} %multiply_multiply_fusion.lap_z, f32[32,8,128]{2,1,0:T(8,128)S(1)} %copy-done.3, f32[4,8,128]{2,1,0:T(8,128)S(1)} %copy-done.4, bf16[2,160,256]{2,1,0:T(8,128)(2,1)S(1)} %copy-done.2, ...), custom_call_target="tpu_custom_call" | custom-call | tf_op jit(solution)/shard_map/final/pallas_call | solution.py:383
  (1 shorter events, 0.0 us)
Async XLA Ops:
  2.9 48.9 %copy-start = (bf16[2,4,256,256]{3,2,1,0:T(8,128)(2,1)S(1)}, bf16[2,4,256,256]{3,2,1,0:T(8,128)(2,1)}, u32[]{:S(2)}) copy-start(bf16[2,4,256,256]{3,2,1,0:T(8,128)(2,1)} %constant.134.clone.dep_any) | copy-start | bytes 3145732
  3.0 48.9 %all-to-all-start = ((f32[256,1,1152]{2,1,0:T(1,128)}), f32[256,1,1152]{2,1,0:T(1,128)S(1)}, u32[]{:S(2)}, u32[]{:S(2)}) async-start(f32[256,1,1152]{2,1,0:T(1,128)} %bitcast.15), calls=%async_computation | async-start | bytes 2359296 | tf_op jit(solution)/shard_map/all_to_all | solution.py:423
  63.4 104.9 %copy-start.1 = (bf16[2,160,256]{2,1,0:T(8,128)(2,1)S(1)}, bf16[2,160,256]{2,1,0:T(8,128)(2,1)}, u32[]{:S(2)}) copy-start(bf16[2,160,256]{2,1,0:T(8,128)(2,1)} %constant.138.clone.cell_low) | copy-start | bytes 491524
  63.4 104.9 %copy-start.2 = (bf16[2,160,256]{2,1,0:T(8,128)(2,1)S(1)}, bf16[2,160,256]{2,1,0:T(8,128)(2,1)}, u32[]{:S(2)}) copy-start(bf16[2,160,256]{2,1,0:T(8,128)(2,1)} %constant.137.clone.cell_high) | copy-start | bytes 491524
  63.4 104.9 %copy-start.3 = (f32[32,8,128]{2,1,0:T(8,128)S(1)}, f32[32,8,128]{2,1,0:T(8,128)}, u32[]{:S(2)}) copy-start(f32[32,8,128]{2,1,0:T(8,128)} %constant.135.clone.lap_x) | copy-start | bytes 393220
  63.5 104.9 %copy-start.4 = (f32[4,8,128]{2,1,0:T(8,128)S(1)}, f32[4,8,128]{2,1,0:T(8,128)}, u32[]{:S(2)}) copy-start(f32[4,8,128]{2,1,0:T(8,128)} %constant.136.clone.lap_y) | copy-start | bytes 49156
  63.5 104.9 %all-to-all-start.1 = ((f32[256,32,128]{2,1,0:T(8,128)}), f32[256,32,128]{2,1,0:T(8,128)}, u32[]{:S(2)}, u32[]{:S(2)}) async-start(f32[256,32,128]{2,1,0:T(8,128)} %middle.1), calls=%async_computation.1 | async-start | bytes 8388608 | tf_op jit(solution)/shard_map/all_to_all | solution.py:425

commit v8 on v7

--- a/solution.py
+++ b/solution.py
@@ -242,10 +242,13 @@
                         flat[pl.ds(at, 128, stride=8), :] = both[
                             ri * 128 : ri * 128 + 128, h * 128 : h * 128 + 128
                         ]
-        leave.append(
-            pltpu.make_async_copy(out.at[k], out_any.at[:, k * 8 : k * 8 + 8, :], sems.at[6 + k])
-        )
-        leave[k].start()
+            rows = slice(half * 128, half * 128 + 128)
+            leave.append(
+                pltpu.make_async_copy(
+                    out.at[k, rows], out_any.at[rows, k * 8 : k * 8 + 8, :], sems.at[6 + k * 2 + half]
+                )
+            )
+            leave[-1].start()
     for copy in leave:
         copy.wait()
 
@@ -273,7 +276,7 @@
             pltpu.VMEM((2 * SLOTS * BRICK, 128), F32),
             pltpu.VMEM((LAYERS, DEVICES, 128), F32),
             pltpu.VMEM((4, DEVICES, 8, 128), F32),
-            pltpu.SemaphoreType.DMA((10,)),
+            pltpu.SemaphoreType.DMA((14,)),
         ],
         compiler_params=pltpu.CompilerParams(vmem_limit_bytes=50 << 20),
         name="middle",

time: 175 us -> 174 us (level)
  no operation moved by 1% of the time
where the time goes in v8:
time: 174 us
  waiting for transfers between devices  130 us (75%)
  starting transfers between devices  23.9 us (14%)
  Pallas kernels  19.5 us (11%)
    all_to_all x1, waiting for transfers between devices, on_device(): pieces = lax.all_to_all(rows, AXES, 0, 0, tiled=True)  96.6 us
    all_to_all x1, waiting for transfers between devices, on_device(): lax.all_to_all(sent.reshape(DEVICES, 1, CHUNK * 128), AXES, 0, 0, tiled=T...  33.1 us
    all_to_all x1, starting transfers between devices, on_device(): lax.all_to_all(sent.reshape(DEVICES, 1, CHUNK * 128), AXES, 0, 0, tiled=T...  15.7 us
    pallas_call x1, Pallas kernels, middle(): pl.pallas_call(middle_kernel, out_shape=jax.ShapeDtypeStruct((DEVICES, 32...  11.3 us
    all_to_all x1, starting transfers between devices, on_device(): pieces = lax.all_to_all(rows, AXES, 0, 0, tiled=True)  8.24 us
    pallas_call x1, Pallas kernels, final(): pl.pallas_call(final_kernel, out_shape=(shape, shape), in_specs=[pl.Block...  5.88 us
  transfers between devices with their start and end apart: 2, of which 2 were waited for; matrix products, arithmetic and copies ran while one was open for 0% of the time, Pallas kernels for 0%

profile of v8, /device:TPU:1, one launch (start us, length us, event | category | flops | bytes accessed | tf_op | source)
XLA Modules:
  0.0 174.2 jit_solution(9105648802579835047)
XLA Ops:
  0.6 2.3 %send.1 = f32[2304,128]{1,0:T(8,128)} custom-call(f32[1024,256]{1,0:T(8,128)} %bitcast.16, s32[2,64]{1,0:T(2,128)} %xy.1, s32[1,4]{1,0:T(1,128)} %bitcast.17), custom_call_target="tpu_custom_call" | custom-call | tf_op jit(solution)/shard_map/send/pallas_call | solution.py:130
  2.9 0.0 copy-start
  3.0 15.7 %all-to-all-start = ((f32[256,1,1152]{2,1,0:T(1,128)}), f32[256,1,1152]{2,1,0:T(1,128)S(1)}, u32[]{:S(2)}, u32[]{:S(2)}) async-start(f32[256,1,1152]{2,1,0:T(1,128)} %bitcast.15), calls=%async_computation | async-start | bytes 2359296 | tf_op jit(solution)/shard_map/all_to_all | solution.py:426
  18.6 0.2 sine_negate_fusion
  18.8 33.1 %all-to-all-done = f32[256,1,1152]{2,1,0:T(1,128)S(1)} async-done(((f32[256,1,1152]{2,1,0:T(1,128)}), f32[256,1,1152]{2,1,0:T(1,128)S(1)}, u32[]{:S(2)}, u32[]{:S(2)}) %all-to-all-start) | async-done | bytes 1179680 | tf_op jit(solution)/shard_map/all_to_all | solution.py:426
  51.9 0.0 copy-done
  51.9 11.3 %middle.1 = f32[256,32,128]{2,1,0:T(8,128)} custom-call(f32[2304,128]{1,0:T(8,128)S(1)} %bitcast.14, f32[2,1024]{1,0:T(2,128)S(1)} %pad_maximum_fusion.twiddle, bf16[4,2,512,512]{3,2,1,0:T(8,128)(2,1)} %constant.133.clone.lat_any, bf16[2,4,256,256]{3,2,1,0:T(8,128)(2,1)S(1)} %copy-done), custom_call_target="tpu_custom_call" | custom-call | tf_op jit(solution)/shard_map/middle/pallas_call | solution.py:260
  63.2 0.0 copy-start.1
  63.2 0.0 copy-start.2
  63.3 0.0 copy-start.3
  63.3 0.0 copy-start.4
  63.3 8.2 %all-to-all-start.1 = ((f32[256,32,128]{2,1,0:T(8,128)}), f32[256,32,128]{2,1,0:T(8,128)}, u32[]{:S(2)}, u32[]{:S(2)}) async-start(f32[256,32,128]{2,1,0:T(8,128)} %middle.1), calls=%async_computation.1 | async-start | bytes 8388608 | tf_op jit(solution)/shard_map/all_to_all | solution.py:428
  71.5 0.1 multiply_multiply_fusion.lap_z
  71.6 96.6 %all-to-all-done.1.pieces_any = f32[256,32,128]{2,1,0:T(8,128)} async-done(((f32[256,32,128]{2,1,0:T(8,128)}), f32[256,32,128]{2,1,0:T(8,128)}, u32[]{:S(2)}, u32[]{:S(2)}) %all-to-all-start.1) | async-done | bytes 4194336 | tf_op jit(solution)/shard_map/all_to_all | solution.py:428
  168.2 0.0 copy-done.1
  168.2 0.0 copy-done.2
  168.2 0.0 copy-done.3
  168.2 0.0 copy-done.4
  168.2 5.9 %final.1 = (f32[2056,128]{1,0:T(8,128)}, f32[2056,128]{1,0:T(8,128)}) custom-call(f32[256,32,128]{2,1,0:T(8,128)} %all-to-all-done.1.pieces_any, f32[2]{0:T(128)S(1)} %multiply_multiply_fusion.lap_z, f32[32,8,128]{2,1,0:T(8,128)S(1)} %copy-done.3, f32[4,8,128]{2,1,0:T(8,128)S(1)} %copy-done.4, bf16[2,160,256]{2,1,0:T(8,128)(2,1)S(1)} %copy-done.2, ...), custom_call_target="tpu_custom_call" | custom-call | tf_op jit(solution)/shard_map/final/pallas_call | solution.py:386
  (1 shorter events, 0.0 us)
Async XLA Ops:
  2.9 48.9 %copy-start = (bf16[2,4,256,256]{3,2,1,0:T(8,128)(2,1)S(1)}, bf16[2,4,256,256]{3,2,1,0:T(8,128)(2,1)}, u32[]{:S(2)}) copy-start(bf16[2,4,256,256]{3,2,1,0:T(8,128)(2,1)} %constant.134.clone.dep_any) | copy-start | bytes 3145732
  3.0 48.9 %all-to-all-start = ((f32[256,1,1152]{2,1,0:T(1,128)}), f32[256,1,1152]{2,1,0:T(1,128)S(1)}, u32[]{:S(2)}, u32[]{:S(2)}) async-start(f32[256,1,1152]{2,1,0:T(1,128)} %bitcast.15), calls=%async_computation | async-start | bytes 2359296 | tf_op jit(solution)/shard_map/all_to_all | solution.py:426
  63.2 104.9 %copy-start.1 = (bf16[2,160,256]{2,1,0:T(8,128)(2,1)S(1)}, bf16[2,160,256]{2,1,0:T(8,128)(2,1)}, u32[]{:S(2)}) copy-start(bf16[2,160,256]{2,1,0:T(8,128)(2,1)} %constant.138.clone.cell_low) | copy-start | bytes 491524
  63.2 104.9 %copy-start.2 = (bf16[2,160,256]{2,1,0:T(8,128)(2,1)S(1)}, bf16[2,160,256]{2,1,0:T(8,128)(2,1)}, u32[]{:S(2)}) copy-start(bf16[2,160,256]{2,1,0:T(8,128)(2,1)} %constant.137.clone.cell_high) | copy-start | bytes 491524
  63.3 104.9 %copy-start.3 = (f32[32,8,128]{2,1,0:T(8,128)S(1)}, f32[32,8,128]{2,1,0:T(8,128)}, u32[]{:S(2)}) copy-start(f32[32,8,128]{2,1,0:T(8,128)} %constant.135.clone.lap_x) | copy-start | bytes 393220
  63.3 104.9 %copy-start.4 = (f32[4,8,128]{2,1,0:T(8,128)S(1)}, f32[4,8,128]{2,1,0:T(8,128)}, u32[]{:S(2)}) copy-start(f32[4,8,128]{2,1,0:T(8,128)} %constant.136.clone.lap_y) | copy-start | bytes 49156
  63.3 104.9 %all-to-all-start.1 = ((f32[256,32,128]{2,1,0:T(8,128)}), f32[256,32,128]{2,1,0:T(8,128)}, u32[]{:S(2)}, u32[]{:S(2)}) async-start(f32[256,32,128]{2,1,0:T(8,128)} %middle.1), calls=%async_computation.1 | async-start | bytes 8388608 | tf_op jit(solution)/shard_map/all_to_all | solution.py:428
